TPU v7x, 256 devices: a whole 4x4x8 slice. The times are simulated.
256 devices in a mesh: wa: 64 (over z, x, core), gy: 4 (over y).
Axes of the slice: x: 4, y: 4, z: 8, core: 2. Of those that a mesh axis runs over, the one named last changes fastest.
Arguments:
- bricks: bfloat16 [1024, 64, 4096], P('wa', None, 'gy'), may hold values from -6 to 6
- brick_coords: int32 [1024, 2], P('wa'), may hold values from 0 to 15, as said below
- counts: int32 [64], P('wa'), may hold values from 1 to 16, as said below
- green_kernel: bfloat16 [64, 2048, 2048], P('wa', 'gy'), may hold values from 0.19921875 to 4
Outputs:
- potential_hat: bfloat16 [64, 2, 2048, 2048], P('wa', None, 'gy')
Inputs may be any that keep to these rules, and one draw needn't show every extreme that they name: Each owner's occupied slots are its first counts[o] slots; in every draw one owner fills all 16. `brick_coords`: column entries are below 2, z bricks below 16; the pairs of one owner's 16 slots are distinct.
All inputs are finite; a program needn't handle non-finite values.
Results may differ from a plain program's by a relative error of at most 0.0072.
Values may be sent and summed in bfloat16 or wider, within the bound.
A program may use at most 128 MiB of HBM per device.

v0:
```python
import math

import jax
import jax.numpy as jnp
from jax import lax
from jax.sharding import PartitionSpec as P

BX = 16
BZ = 16
COL_DEV = 2


def twiddle(positions, frequency, length, factor):
    product = positions[:, None] * frequency[None, :] % length
    angles = product.astype(jnp.float32) * (2.0 * math.pi / length)
    return (
        (jnp.cos(angles) * factor).astype(jnp.bfloat16),
        (jnp.sin(angles) * factor).astype(jnp.bfloat16),
    )


def on_device(bricks, brick_coords, counts, green_kernel):
    depth_count, kx_count, length = green_kernel.shape
    owners = lax.axis_size("wa")
    groups = lax.axis_size("gy")
    depth_total = depth_count * owners
    slot_count, brick_edge, cell_count = bricks.shape
    rows_brick = cell_count // brick_edge
    frequency = jnp.arange(depth_total, dtype=jnp.int32)
    depth_cosine, depth_sine = twiddle(
        jnp.arange(brick_edge, dtype=jnp.int32), frequency, length, 1.0 / math.sqrt(BZ * brick_edge)
    )
    depth_table = jnp.concatenate([depth_cosine.T, -depth_sine.T], 0)
    raw_terms = jnp.einsum("qz,szc->qsc", depth_table, bricks, preferred_element_type=jnp.float32)
    raw_terms = raw_terms.reshape(2, depth_total, slot_count, cell_count)
    angles = (frequency[:, None] * (brick_coords[None, :, 1] * brick_edge) % length).astype(
        jnp.float32
    ) * (2.0 * math.pi / length)
    cosine = jnp.cos(angles)[:, :, None]
    sine_part = jnp.sin(angles)[:, :, None]
    alive_mask = (jnp.arange(slot_count, dtype=jnp.int32) < counts[0]).astype(jnp.float32)[
        None, :, None
    ]
    real_part = raw_terms[0]
    imag_part = raw_terms[1]
    rotated = jnp.stack(
        [
            (real_part * cosine + imag_part * sine_part) * alive_mask,
            (imag_part * cosine - real_part * sine_part) * alive_mask,
        ],
        0,
    )
    column_total = COL_DEV * owners
    arrived = lax.all_to_all(rotated, "wa", split_axis=1, concat_axis=2, tiled=True)
    local_ids = lax.all_gather(brick_coords[:, 0], "wa", axis=0, tiled=True).reshape(
        owners, slot_count
    )
    arrived = arrived.reshape(2, depth_count, owners, slot_count, cell_count)
    pieces = []
    for position in range(COL_DEV):
        chosen = (local_ids == position).astype(jnp.float32)[None, None, :, :, None]
        pieces.append(jnp.sum(arrived * chosen, axis=3))
    gathered = jnp.stack(pieces, 3).reshape(2, depth_count, column_total, cell_count)
    spectra = gathered.astype(jnp.bfloat16)
    brick_rows = column_total // BX
    local_rows = brick_rows * rows_brick
    layout = spectra.reshape(2, depth_count, brick_rows, BX, rows_brick, brick_edge)
    layout = layout.transpose(0, 1, 2, 4, 3, 5).reshape(2, depth_count, local_rows, BX * brick_edge)
    across_cosine, across_sine = twiddle(
        jnp.arange(BX * brick_edge, dtype=jnp.int32),
        jnp.arange(length, dtype=jnp.int32),
        length,
        1.0 / math.sqrt(BX * brick_edge),
    )
    across_real = jnp.einsum(
        "kyx,xq->kyq", layout[0], across_cosine, preferred_element_type=jnp.float32
    ) + jnp.einsum("kyx,xq->kyq", layout[1], across_sine, preferred_element_type=jnp.float32)
    across_imag = jnp.einsum(
        "kyx,xq->kyq", layout[1], across_cosine, preferred_element_type=jnp.float32
    ) - jnp.einsum("kyx,xq->kyq", layout[0], across_sine, preferred_element_type=jnp.float32)
    planes = jnp.stack([across_real, across_imag], 0).astype(jnp.bfloat16)
    regrouped = lax.all_to_all(planes, "gy", split_axis=3, concat_axis=2, tiled=True)
    rows_every = jnp.arange(groups * local_rows, dtype=jnp.int32)
    source = rows_every // local_rows
    within = rows_every % local_rows
    global_rows = within // rows_brick * brick_edge + source * rows_brick + within % rows_brick
    rows_cosine, rows_sine = twiddle(
        global_rows,
        jnp.arange(length, dtype=jnp.int32),
        length,
        1.0 / math.sqrt(brick_rows * brick_edge),
    )
    final_real = jnp.einsum(
        "kyx,yq->kxq", regrouped[0], rows_cosine, preferred_element_type=jnp.float32
    ) + jnp.einsum("kyx,yq->kxq", regrouped[1], rows_sine, preferred_element_type=jnp.float32)
    final_imag = jnp.einsum(
        "kyx,yq->kxq", regrouped[1], rows_cosine, preferred_element_type=jnp.float32
    ) - jnp.einsum("kyx,yq->kxq", regrouped[0], rows_sine, preferred_element_type=jnp.float32)
    weights = green_kernel.astype(jnp.float32)
    return jnp.stack([weights * final_real, weights * final_imag], 1).astype(jnp.bfloat16)


def solution(mesh):
    return jax.shard_map(
        on_device,
        mesh=mesh,
        in_specs=(P("wa", None, "gy"), P("wa", None), P("wa"), P("wa", "gy", None)),
        out_specs=P("wa", None, "gy", None),
        check_vma=False,
    )
```

profile of v0, /device:TPU:4, one launch (start us, length us, event | category | flops | bytes accessed | tf_op | source)
XLA Modules:
  0.0 447.8 jit_solution(4219671998319276366)
XLA Ops:
  0.0 0.1 fusion.34
  0.2 0.1 multiply_convert_fusion.25
  0.3 0.8 multiply_bitcast_fusion.2
  1.9 1.3 fusion.35
  3.3 1.4 multiply_bitcast_fusion.1
  4.7 1.7 pad_maximum_fusion
  6.3 8.1 %copy.29 = f32[2,64,16,1024]{3,2,0,1:T(8,128)} copy(f32[2,64,16,1024]{3,1,2,0:T(8,128)S(1)} %pad_maximum_fusion) | data formatting | bytes 16777216 | tf_op jit(solution)/shard_map/stack | solution.py:46
  14.4 12.3 %all-to-all-start = ((f32[2,64,16,1024]{3,2,0,1:T(8,128)}), f32[2,64,16,1024]{3,2,0,1:T(8,128)}, u32[]{:S(2)}, u32[]{:S(2)}) async-start(f32[2,64,16,1024]{3,2,0,1:T(8,128)} %copy.29), calls=%async_computation | async-start | bytes 16777216 | tf_op jit(solution)/shard_map/all_to_all | solution.py:54
  26.8 0.6 dynamic-slice
  28.1 189.9 %all-reduce = s32[1024]{0:T(1024)S(1)} all-reduce(s32[1024]{0:T(1024)S(1)} %bitcast_dynamic-update-slice_fusion), channel_id=2, replica_groups=mesh['wa'=64,'gy'=4] {'wa'}, use_global_device_ids=true, to_apply=%add | all-reduce | flops 1024 | bytes 8192
  218.2 8.2 %multiply_reduce_fusion.1 = (bf16[2,64,1024]{2,0,1:T(2,128)(2,1)S(1)}, bf16[2,64,1024]{2,0,1:T(2,128)(2,1)S(1)}) fusion(f32[2,64,16,1024]{3,2,0,1:T(8,128)} %all-to-all-done, f32[64,16]{1,0:T(8,128)S(1)} %reshape.299, f32[64,16]{1,0:T(8,128)S(1)} %reshape.300), kind=kLoop, calls=%fused_computation.12 | loop fusion | flops 8126464 | bytes 8921088 | tf_op jit(solution)/shard_map/reduce_sum | solution.py:62
  226.6 0.5 copy.32
  227.1 0.6 convert_element_type.134
  227.7 0.2 fusion.101
  228.0 0.1 copy.33
  228.1 0.3 reshape.295
  228.5 32.1 %fusion.14 = f32[128,2048]{1,0:T(8,128)S(1)} fusion(bf16[128,1024]{1,0:T(8,128)(2,1)S(1)} %reshape.295), kind=kOutput, calls=%fused_computation.30 | convolution fusion | flops 570425344 | bytes 1310720 | tf_op jit(solution)/shard_map/kyx,xq->kyq/dot_general | solution.py:75
  260.5 0.1 copy.34
  260.7 0.3 reshape.296
  261.0 32.3 %fusion.13 = f32[128,2048]{1,0:T(8,128)S(1)} fusion(bf16[128,1024]{1,0:T(8,128)(2,1)S(1)} %reshape.296), kind=kOutput, calls=%fused_computation.29 | convolution fusion | flops 570425344 | bytes 1310720 | tf_op jit(solution)/shard_map/kyx,xq->kyq/dot_general | solution.py:78
  293.3 32.4 %fusion.24 = bf16[1,1,128,2048]{3,2,1,0:T(8,128)(2,1)S(1)} fusion(f32[128,2048]{1,0:T(8,128)S(1)} %fusion.14, bf16[128,1024]{1,0:T(8,128)(2,1)S(1)} %reshape.296), kind=kOutput, calls=%fused_computation.42 | convolution fusion | flops 570949632 | bytes 1835008 | tf_op jit(solution)/shard_map/kyx,xq->kyq/dot_general | solution.py:77
  325.7 32.4 %fusion.25 = bf16[1,1,128,2048]{3,2,1,0:T(8,128)(2,1)S(1)} fusion(f32[128,2048]{1,0:T(8,128)S(1)} %fusion.13, bf16[128,1024]{1,0:T(8,128)(2,1)S(1)} %reshape.295), kind=kOutput, calls=%fused_computation.43 | convolution fusion | flops 570949632 | bytes 1835008 | tf_op jit(solution)/shard_map/kyx,xq->kyq/dot_general | solution.py:80
  358.2 2.0 copy.35
  360.2 4.9 %all-to-all-start.1 = ((bf16[2,1,128,2048]{2,0,1,3:T(2,128)(2,1)}), bf16[2,1,128,2048]{2,0,1,3:T(2,128)(2,1)S(1)}, u32[]{:S(2)}, u32[]{:S(2)}) async-start(bf16[2,1,128,2048]{2,0,1,3:T(2,128)(2,1)} %copy.35), calls=%async_computation.1 | async-start | bytes 2097152 | tf_op jit(solution)/shard_map/all_to_all | solution.py:82
  365.1 12.9 %all-to-all-done.1 = bf16[2,1,128,2048]{2,0,1,3:T(2,128)(2,1)S(1)} async-done(((bf16[2,1,128,2048]{2,0,1,3:T(2,128)(2,1)}), bf16[2,1,128,2048]{2,0,1,3:T(2,128)(2,1)S(1)}, u32[]{:S(2)}, u32[]{:S(2)}) %all-to-all-start.1) | async-done | bytes 1048608 | tf_op jit(solution)/shard_map/all_to_all | solution.py:82
  378.2 0.2 copy.37
  378.5 0.2 copy.38
  378.7 16.1 %fusion.27 = f32[512,2048]{1,0:T(8,128)S(1)} fusion(bf16[512,512]{1,0:T(8,128)(2,1)S(1)} %bitcast.57, s32[512]{0:T(512)S(1)} %fusion.52), kind=kOutput, calls=%fused_computation.45 | convolution fusion | flops 1090519040 | bytes 4720640 | tf_op jit(solution)/shard_map/kyx,yq->kxq/dot_general | solution.py:93
  394.8 16.2 %fusion.26 = f32[512,2048]{1,0:T(8,128)S(1)} fusion(bf16[512,512]{1,0:T(8,128)(2,1)S(1)} %bitcast.59, s32[512]{0:T(512)S(1)} %fusion.52), kind=kOutput, calls=%fused_computation.44 | convolution fusion | flops 1090519040 | bytes 4720640 | tf_op jit(solution)/shard_map/kyx,yq->kxq/dot_general | solution.py:96
  411.0 17.2 %fusion.19 = bf16[1,1,512,2048]{3,2,1,0:T(8,128)(2,1)S(1)} fusion(f32[512,2048]{1,0:T(8,128)S(1)} %fusion.27, bf16[512,512]{1,0:T(8,128)(2,1)S(1)} %bitcast.60, bf16[1,512,2048]{2,1,0:T(8,128)(2,1)S(1)} %copy-done.2, s32[512]{0:T(512)S(1)} %fusion.52), kind=kOutput, calls=%fused_computation.37 | convolution fusion | flops 1094713344 | bytes 8914944 | tf_op jit(solution)/shard_map/kyx,yq->kxq/dot_general | solution.py:95
  428.2 16.9 %fusion.18 = bf16[1,1,512,2048]{3,2,1,0:T(8,128)(2,1)S(1)} fusion(f32[512,2048]{1,0:T(8,128)S(1)} %fusion.26, bf16[512,512]{1,0:T(8,128)(2,1)S(1)} %bitcast.58, bf16[1,512,2048]{2,1,0:T(8,128)(2,1)S(1)} %copy-done.2, s32[512]{0:T(512)S(1)} %fusion.52), kind=kOutput, calls=%fused_computation.36 | convolution fusion | flops 1094713344 | bytes 8914944 | tf_op jit(solution)/shard_map/kyx,yq->kxq/dot_general | solution.py:98
  445.2 2.4 pad_maximum_fusion.1
  (24 shorter events, 0.9 us)
Async XLA Ops:
  0.0 1.9 copy-start
  14.4 12.3 %copy-start.4 = (u32[256]{0:T(256)S(1)}, u32[256]{0:T(256)}, u32[]{:S(2)}) copy-start(u32[256]{0:T(256)} %constant.113) | copy-start | bytes 3076
  14.4 13.6 %copy-start.3 = (s32[16,2]{0,1:T(2,128)S(1)}, s32[16,2]{0,1:T(2,128)}, u32[]{:S(2)}) copy-start(s32[16,2]{0,1:T(2,128)} %param.5) | copy-start | bytes 388
  14.4 203.7 %all-to-all-start = ((f32[2,64,16,1024]{3,2,0,1:T(8,128)}), f32[2,64,16,1024]{3,2,0,1:T(8,128)}, u32[]{:S(2)}, u32[]{:S(2)}) async-start(f32[2,64,16,1024]{3,2,0,1:T(8,128)} %copy.29), calls=%async_computation | async-start | bytes 16777216 | tf_op jit(solution)/shard_map/all_to_all | solution.py:54
  360.2 17.9 %all-to-all-start.1 = ((bf16[2,1,128,2048]{2,0,1,3:T(2,128)(2,1)}), bf16[2,1,128,2048]{2,0,1,3:T(2,128)(2,1)S(1)}, u32[]{:S(2)}, u32[]{:S(2)}) async-start(bf16[2,1,128,2048]{2,0,1,3:T(2,128)(2,1)} %copy.35), calls=%async_computation.1 | async-start | bytes 2097152 | tf_op jit(solution)/shard_map/all_to_all | solution.py:82
  394.8 16.2 %copy-start.2 = (bf16[1,512,2048]{2,1,0:T(8,128)(2,1)S(1)}, bf16[1,512,2048]{2,1,0:T(8,128)(2,1)}, u32[]{:S(2)}) copy-start(bf16[1,512,2048]{2,1,0:T(8,128)(2,1)} %param.7) | copy-start | bytes 6291460
  428.2 19.3 %copy-start.1 = (bf16[16,64,1024]{2,1,0:T(8,128)(2,1)S(1)}, bf16[16,64,1024]{2,1,0:T(8,128)(2,1)}, u32[]{:S(2)}) copy-start(bf16[16,64,1024]{2,1,0:T(8,128)(2,1)} %param.4) | copy-start | bytes 6291460
where the time goes:
time: 455 us; the launch traced here: 448 us
  matrix products  197 us (43%)
  blocking collectives  190 us (42%)
  starting transfers between devices  17.2 us (4%)
  other arithmetic  15 us (3%)
  local copies, waits for them, and re-layouts  14 us (3%)
  waiting for transfers between devices  13 us (3%)
    unnamed x1, blocking collectives  190 us
    dot_general x1, matrix products, on_device(): jnp.einsum('kyx,xq->kyq', layout[0], across_sine, preferred_element_type=...  32.4 us
    dot_general x1, matrix products, on_device(): jnp.einsum('kyx,xq->kyq', layout[1], across_sine, preferred_element_type=...  32.4 us
    dot_general x1, matrix products, on_device(): jnp.einsum('kyx,xq->kyq', layout[1], across_cosine, preferred_element_typ...  32.3 us
    dot_general x1, matrix products, on_device(): jnp.einsum('kyx,xq->kyq', layout[0], across_cosine, preferred_element_typ...  32.1 us
    dot_general x1, matrix products, on_device(): jnp.einsum('kyx,yq->kxq', regrouped[1], rows_sine, preferred_element_type...  17.2 us
    dot_general x1, matrix products, on_device(): jnp.einsum('kyx,yq->kxq', regrouped[0], rows_sine, preferred_element_type...  16.9 us
    dot_general x1, matrix products, on_device(): jnp.einsum('kyx,yq->kxq', regrouped[1], rows_cosine, preferred_element_ty...  16.2 us
  transfers between devices with their start and end apart: 2, of which 1 were waited for; matrix products, arithmetic and copies ran while one was open for 0% of the time, Pallas kernels for 0%

commit v1 on v0

v1 whole, which is shorter than its diff:
```python
import math

import jax
import jax.numpy as jnp
import ml_dtypes
import numpy as np
from jax import lax
from jax.sharding import PartitionSpec as P

BX = 16
BZ = 16
COL_DEV = 2


def wave(positions, frequency, length, factor):
    angles = (positions[:, None] * frequency[None, :] % length) * (2.0 * math.pi / length)
    return (np.cos(angles) * factor).astype(ml_dtypes.bfloat16), (np.sin(angles) * factor).astype(ml_dtypes.bfloat16)


def on_device(bricks, brick_coords, counts, green_kernel):
    depth_count, kx_count, length = green_kernel.shape
    owners = lax.axis_size("wa")
    groups = lax.axis_size("gy")
    depth_total = depth_count * owners
    slot_count, edge, cells = bricks.shape
    rows_brick = cells // edge
    depth_cosine, depth_sine = wave(np.arange(BZ * edge), np.arange(depth_total), length, 1.0 / math.sqrt(BZ * edge))
    table = np.concatenate([depth_cosine, (-depth_sine.astype(np.float32)).astype(ml_dtypes.bfloat16)], 1)
    table = jnp.asarray(table.reshape(BZ, edge, 2 * depth_total).transpose(0, 2, 1))
    picked = jnp.take(table, brick_coords[:, 1], axis=0)
    alive = jnp.arange(slot_count, dtype=jnp.int32) < counts[0]
    mine = (brick_coords[:, 0][None, :] == jnp.arange(COL_DEV, dtype=jnp.int32)[:, None]) & alive[None, :]
    mixing = picked[None] * mine[:, :, None, None].astype(jnp.bfloat16)
    sums = jnp.einsum("gsqz,szc->gqc", mixing, bricks, preferred_element_type=jnp.float32)
    spectra = sums.astype(jnp.bfloat16).reshape(COL_DEV, 2, depth_total, rows_brick, edge)
    spectra = spectra.transpose(2, 1, 3, 0, 4).reshape(depth_total, 2, rows_brick, COL_DEV * edge)
    arrived = lax.all_to_all(spectra, "wa", split_axis=0, concat_axis=0, tiled=True)
    wide = BX // COL_DEV
    brick_rows = owners // wide
    local_rows = brick_rows * rows_brick
    layout = arrived.reshape(brick_rows, wide, 2, rows_brick, COL_DEV * edge)
    layout = layout.transpose(2, 0, 3, 1, 4).reshape(2, local_rows, BX * edge)
    cosine, sine = wave(np.arange(BX * edge), np.arange(length), length, 1.0 / math.sqrt(BX * edge))
    negative = (-sine.astype(np.float32)).astype(ml_dtypes.bfloat16)
    both = jnp.asarray(np.stack([np.stack([cosine, sine]), np.stack([negative, cosine])], 0))
    planes = jnp.einsum("pyx,opxq->oyq", layout, both, preferred_element_type=jnp.float32).astype(jnp.bfloat16)
    regrouped = lax.all_to_all(planes, "gy", split_axis=2, concat_axis=1, tiled=True)
    every = np.arange(groups * local_rows)
    source, within = every // local_rows, every % local_rows
    global_rows = within // rows_brick * edge + source * rows_brick + within % rows_brick
    cosine, sine = wave(global_rows, np.arange(length), length, 1.0 / math.sqrt(brick_rows * edge))
    negative = (-sine.astype(np.float32)).astype(ml_dtypes.bfloat16)
    both = jnp.asarray(np.stack([np.stack([cosine, sine]), np.stack([negative, cosine])], 0))
    final = jnp.einsum("pyx,opyr->oxr", regrouped, both, preferred_element_type=jnp.float32)
    return (final * green_kernel.astype(jnp.float32)).astype(jnp.bfloat16)[None]


def solution(mesh):
    return jax.shard_map(
        on_device,
        mesh=mesh,
        in_specs=(P("wa", None, "gy"), P("wa", None), P("wa"), P("wa", "gy", None)),
        out_specs=P("wa", None, "gy", None),
        check_vma=False,
    )
```

time: 455 us -> 86.7 us (0.19)
  the two profiles are of different devices: /device:TPU:4 before, /device:TPU:1 now
where the time goes in v1:
time: 86.7 us; the launch traced here: 86.4 us
  blocking collectives  30.5 us (35%)
  matrix products  20 us (23%)
  local copies, waits for them, and re-layouts  14.8 us (17%)
  waiting for transfers between devices  10.4 us (12%)
  other arithmetic  5.76 us (7%)
  starting transfers between devices  4.18 us (5%)
    all_to_all x1, blocking collectives, on_device(): lax.all_to_all(spectra, 'wa', split_axis=0, concat_axis=0, tiled=True)  30.5 us
    all_to_all x1, waiting for transfers between devices, on_device(): lax.all_to_all(planes, 'gy', split_axis=2, concat_axis=1, tiled=True)  10.4 us
    dot_general x1, matrix products, on_device(): jnp.einsum('pyx,opyr->oxr', regrouped, both, preferred_element_type=jnp.f...  10.1 us
    dot_general x1, matrix products, on_device(): jnp.einsum('pyx,opxq->oyq', layout, both, preferred_element_type=jnp.floa...  8.29 us
    reshape x2, local copies, waits for them, and re-layouts, on_device(): sums.astype(jnp.bfloat16).reshape(COL_DEV, 2, depth_total, rows_brick, edge)  4.34 us
    all_to_all x1, starting transfers between devices, on_device(): lax.all_to_all(planes, 'gy', split_axis=2, concat_axis=1, tiled=True)  4.18 us
    mul x1, other arithmetic, on_device(): return (final * green_kernel.astype(jnp.float32)).astype(jnp.bfloat16)[None]  4.06 us
    all_to_all x2, local copies, waits for them, and re-layouts, on_device(): lax.all_to_all(planes, 'gy', split_axis=2, concat_axis=1, tiled=True)  3.25 us
  transfers between devices with their start and end apart: 1, of which 1 were waited for; matrix products, arithmetic and copies ran while one was open for 5% of the time, Pallas kernels for 0%

profile of v1, /device:TPU:1, one launch (start us, length us, event | category | flops | bytes accessed | tf_op | source)
XLA Modules:
  0.0 86.4 jit_solution(8450380916489983388)
XLA Ops:
  0.0 0.0 copy-start
  0.0 0.8 and_bitcast_fusion
  0.8 0.8 fusion.15
  2.3 1.5 %gather_fusion = bf16[16,128,64]{1,2,0:T(8,128)(2,1)S(1)} fusion(bf16[16,128,64]{1,2,0:T(8,128)(2,1)} %constant.22.clone, s32[1024]{0:T(1024)S(1)} %pad_clamp_fusion), kind=kCustom, calls=%fused_computation | custom fusion | bytes 524352 | tf_op jit(solution)/shard_map/jit(_take)/gather | solution.py:30
  3.8 0.1 broadcast_select_fusion
  3.9 0.0 copy-done
  4.0 1.6 %fusion.9 = bf16[2,128,1024]{2,1,0:T(8,128)(2,1)} fusion(bf16[16,64,1024]{2,1,0:T(8,128)(2,1)S(1)} %copy-done, bf16[2,16]{1,0:T(2,128)(2,1)S(1)} %and_convert_fusion, bf16[16,128,64]{1,2,0:T(8,128)(2,1)S(1)} %broadcast_select_fusion), kind=kOutput, calls=%fused_computation.11 | convolution fusion | flops 537395200 | bytes 2883648 | tf_op jit(solution)/shard_map/gsqz,szc->gqc/dot_general | solution.py:34
  5.6 1.8 %reshape.58 = bf16[2,2,64,16,64]{4,3,2,1,0:T(8,128)(2,1)S(1)} reshape(bf16[2,128,1024]{2,1,0:T(8,128)(2,1)} %fusion.9) | data formatting | bytes 1048576 | tf_op jit(solution)/shard_map/reshape | solution.py:35
  7.3 2.6 %copy.22 = bf16[2,2,64,16,64]{4,0,3,1,2:T(2,128)(2,1)} copy(bf16[2,2,64,16,64]{4,3,2,1,0:T(8,128)(2,1)S(1)} %reshape.58) | data formatting | bytes 1048576 | tf_op jit(solution)/shard_map/reshape | solution.py:35
  9.9 2.4 %reshape.59 = bf16[64,2,16,128]{3,2,1,0:T(8,128)(2,1)S(1)} reshape(bf16[64,2,16,2,64]{4,3,2,1,0:T(2,128)(2,1)} %bitcast.62) | data formatting | bytes 1048576 | tf_op jit(solution)/shard_map/reshape | solution.py:36
  12.3 30.5 %all_to_all.23 = bf16[64,2,16,128]{3,2,1,0:T(8,128)(2,1)S(1)} all-to-all(bf16[64,2,16,128]{3,2,1,0:T(8,128)(2,1)S(1)} %reshape.59), channel_id=1, replica_groups=mesh['wa'=64,'gy'=4] {'wa'}, dimensions={0} | all-to-all | bytes 1048576 | tf_op jit(solution)/shard_map/all_to_all | solution.py:37
  42.8 0.2 copy.13
  43.0 1.0 %reshape.73 = bf16[2,128,1024,1]{2,1,0,3:T(8,128)(2,1)} reshape(bf16[2,8,16,8,128]{4,3,2,1,0:T(8,128)(2,1)S(1)} %copy.13) | data formatting | bytes 1048576 | tf_op jit(solution)/shard_map/reshape | solution.py:42
  44.1 8.3 %fusion.3 = bf16[2,128,2048]{2,1,0:T(8,128)(2,1)S(1)} fusion(bf16[2,128,1024,1]{2,1,0,3:T(8,128)(2,1)} %reshape.73, bf16[2,2,1024,2048]{3,2,1,0:T(8,128)(2,1)} %constant.23.clone), kind=kOutput, calls=%fused_computation.6 | convolution fusion | flops 2148007936 | bytes 18350080 | tf_op jit(solution)/shard_map/pyx,opxq->oyq/dot_general | solution.py:46
  52.4 2.0 %copy.14 = bf16[2,128,2048]{1,0,2:T(2,128)(2,1)} copy(bf16[2,128,2048]{2,1,0:T(8,128)(2,1)S(1)} %fusion.3) | data formatting | bytes 2097152 | tf_op jit(solution)/shard_map/convert_element_type | solution.py:46
  54.4 4.2 %all-to-all-start.1 = ((bf16[2,128,2048]{1,0,2:T(2,128)(2,1)}), bf16[2,128,2048]{1,0,2:T(2,128)(2,1)S(1)}, u32[]{:S(2)}, u32[]{:S(2)}) async-start(bf16[2,128,2048]{1,0,2:T(2,128)(2,1)} %copy.14), calls=%async_computation.1 | async-start | bytes 2097152 | tf_op jit(solution)/shard_map/all_to_all | solution.py:47
  58.5 4.1 %bitcast_convert_fusion = f32[512,2048]{1,0:T(8,128)} fusion(bf16[1,512,2048]{2,1,0:T(8,128)(2,1)} %param.10), kind=kLoop, calls=%fused_computation.7 | loop fusion | flops 1048576 | bytes 6291456 | tf_op jit(solution)/shard_map/mul | solution.py:55
  62.6 10.4 %all-to-all-done.1 = bf16[2,128,2048]{1,0,2:T(2,128)(2,1)S(1)} async-done(((bf16[2,128,2048]{1,0,2:T(2,128)(2,1)}), bf16[2,128,2048]{1,0,2:T(2,128)(2,1)S(1)}, u32[]{:S(2)}, u32[]{:S(2)}) %all-to-all-start.1) | async-done | bytes 1048608 | tf_op jit(solution)/shard_map/all_to_all | solution.py:47
  73.0 1.8 %copy.21 = bf16[2,128,4,512]{1,2,3,0:T(4,128)(2,1)} copy(bf16[2,128,4,512]{1,0,3,2:T(2,128)(2,1)S(1)} %bitcast.61) | data formatting | bytes 2097152 | tf_op jit(solution)/shard_map/all_to_all | solution.py:47
  74.8 1.5 %reshape.75 = bf16[2,512,512,1]{1,2,0,3:T(8,128)(2,1)S(1)} reshape(bf16[2,4,128,512]{2,1,3,0:T(4,128)(2,1)} %bitcast.63) | data formatting | bytes 2097152 | tf_op jit(solution)/shard_map/all_to_all | solution.py:47
  76.3 10.1 %fusion.1 = bf16[1,2,512,2048]{3,2,1,0:T(8,128)(2,1)} fusion(f32[512,2048]{1,0:T(8,128)} %bitcast_convert_fusion, bf16[2,512,512,1]{1,2,0,3:T(8,128)(2,1)S(1)} %reshape.75, bf16[2,2,512,2048]{3,2,1,0:T(8,128)(2,1)} %constant.24.clone), kind=kOutput, calls=%fused_computation.3 | convolution fusion | flops 4299161600 | bytes 17825792 | tf_op jit(solution)/shard_map/pyx,opyr->oxr/dot_general | solution.py:54
  (3 shorter events, 0.0 us)
Async XLA Ops:
  0.0 3.9 %copy-start = (bf16[16,64,1024]{2,1,0:T(8,128)(2,1)S(1)}, bf16[16,64,1024]{2,1,0:T(8,128)(2,1)}, u32[]{:S(2)}) copy-start(bf16[16,64,1024]{2,1,0:T(8,128)(2,1)} %param.7) | copy-start | bytes 6291460
  54.4 18.7 %all-to-all-start.1 = ((bf16[2,128,2048]{1,0,2:T(2,128)(2,1)}), bf16[2,128,2048]{1,0,2:T(2,128)(2,1)S(1)}, u32[]{:S(2)}, u32[]{:S(2)}) async-start(bf16[2,128,2048]{1,0,2:T(2,128)(2,1)} %copy.14), calls=%async_computation.1 | async-start | bytes 2097152 | tf_op jit(solution)/shard_map/all_to_all | solution.py:47

commit v2 on v1

v2 whole, which is shorter than its diff:
```python
import functools
import math

import jax
import jax.numpy as jnp
import ml_dtypes
import numpy as np
from jax import lax
from jax.experimental import pallas as pl
from jax.experimental.pallas import tpu as pltpu
from jax.sharding import PartitionSpec as P

BX = 16
BZ = 16
COL_DEV = 2
MESH = pl.DeviceIdType.MESH
LANES = 128


def wave(positions, frequency, length, factor):
    angles = (positions[:, None] * frequency[None, :] % length) * (2.0 * math.pi / length)
    return np.cos(angles) * factor, np.sin(angles) * factor


def constant(array):
    return jnp.asarray(array.astype(ml_dtypes.bfloat16))


def quarter_turn(value):
    lane = lax.broadcasted_iota(jnp.int32, value.shape, value.ndim - 1) % LANES
    turned = jnp.concatenate(
        [pltpu.roll(value[:, at : at + LANES], LANES // 2, 1) for at in range(0, value.shape[1], LANES)], 1
    )
    return jnp.where(lane < LANES // 2, turned, -turned)


def exchange(
    coords, counts, bricks_hbm, depth_hbm, weave_hbm, gather_hbm, across_hbm, out,
    bricks, depth, weave, gather, across, mixing, spread, blocks, plane, parts, result,
    load_sem, send_sem, recv_sem, own_sem, send_sem2, recv_sem2, own_sem2,
):
    owners, groups = lax.axis_size("wa"), lax.axis_size("gy")
    me, my = lax.axis_index("wa"), lax.axis_index("gy")
    slots = coords.shape[0]
    wide = BX // COL_DEV
    loads = [
        pltpu.make_async_copy(source, target, load_sem.at[i])
        for i, (source, target) in enumerate(
            [(depth_hbm, depth), (bricks_hbm, bricks), (weave_hbm, weave), (gather_hbm, gather), (across_hbm, across)]
        )
    ]
    for load in loads:
        load.start()
    barrier = pltpu.get_barrier_semaphore()

    def greet(step, carry):
        pl.semaphore_signal(barrier, inc=1, device_id=((me + step) % owners, my), device_id_type=MESH)
        return carry

    lax.fori_loop(1, owners, greet, 0)
    for step in range(1, groups):
        pl.semaphore_signal(barrier, inc=1, device_id=(me, (my + step) % groups), device_id_type=MESH)

    loads[0].wait()
    lane = lax.broadcasted_iota(jnp.int32, (1, LANES), 1)
    for pair in range(slots // 2):
        first, second = 2 * pair, 2 * pair + 1
        picked = jnp.where(lane < LANES // 2, depth[coords[first, 1]], depth[coords[second, 1]])
        for column in range(COL_DEV):
            keep = [
                jnp.where(jnp.logical_and(coords[s, 0] == column, s < counts[0]), 1.0, 0.0).astype(jnp.float32)
                for s in (first, second)
            ]
            mask = jnp.where(lane < LANES // 2, keep[0], keep[1]).astype(jnp.bfloat16)
            mixing[column * LANES : (column + 1) * LANES, pair * LANES : (pair + 1) * LANES] = picked * mask
    loads[1].wait()
    loads[2].wait()
    wave_count = LANES // 2
    for quad in range(4):
        sums = jnp.dot(mixing[...], bricks[:, quad * 256 : (quad + 1) * 256], preferred_element_type=jnp.float32)
        sums = sums.astype(jnp.bfloat16)
        rows = [
            jnp.concatenate([sums[:LANES, at : at + LANES], sums[LANES:, at : at + LANES]], 1) for at in (0, LANES)
        ]
        woven = jnp.dot(jnp.concatenate(rows, 0), weave[...], preferred_element_type=jnp.float32)
        for pair in range(2):
            for part in range(2):
                for parity in range(2):
                    start = pair * LANES + part * wave_count
                    spread[pl.ds(parity * 16 + part * 8 + quad * 2 + pair, wave_count, stride=32), :] = woven[
                        start : start + wave_count, parity * LANES : (parity + 1) * LANES
                    ]
    blocks[...] = spread[...].astype(jnp.bfloat16).reshape(blocks.shape)

    def place(source):
        rows = pl.multiple_of(source // wide * 8, 8)
        columns = pl.multiple_of(source % wide * LANES, LANES)
        return plane.at[:, :, pl.ds(rows, 8), pl.ds(columns, LANES)]

    own = pltpu.make_async_copy(blocks.at[me], place(me), own_sem)
    own.start()
    pl.semaphore_wait(barrier, owners - 1 + groups - 1)

    def send(step, carry):
        target = (me + step) % owners
        pltpu.make_async_remote_copy(
            blocks.at[target], place(me), send_sem.at[step], recv_sem.at[step], (target, my), MESH
        ).start()
        return carry

    lax.fori_loop(1, owners, send, 0)
    own.wait()

    def receive(step, carry):
        source = (me + owners - step) % owners
        pltpu.make_async_remote_copy(
            blocks.at[source], place(source), send_sem.at[step], recv_sem.at[step], (source, my), MESH
        ).wait_recv()
        return carry

    lax.fori_loop(1, owners, receive, 0)
    loads[3].wait()
    loads[4].wait()
    for half in range(2):
        piece = plane[:, :, :, half * 512 : (half + 1) * 512].reshape(256, 512)
        sorted_ = jnp.dot(piece, gather[...], preferred_element_type=jnp.float32)
        turned = jnp.concatenate([sorted_[64:128], -sorted_[:64], sorted_[192:], -sorted_[128:192]], 0)
        for m in range(4):
            at = half * LANES
            parts[m, :, at : at + LANES] = sorted_[:, m * LANES : (m + 1) * LANES].astype(jnp.bfloat16)
            parts[m, :, 256 + at : 256 + at + LANES] = turned[:, m * LANES : (m + 1) * LANES].astype(jnp.bfloat16)
    chunk = 128
    chunks = across.shape[1] // chunk

    def outgoing(step, at):
        target = (my + step) % groups
        rows = pl.ds(at * chunk, chunk)
        return pltpu.make_async_remote_copy(
            result.at[target, :, rows, :],
            out.at[:, rows, pl.ds(pl.multiple_of(my * LANES, LANES), LANES)],
            send_sem2.at[step, at],
            recv_sem2.at[step, at],
            (me, target),
            MESH,
        )

    def incoming(step, at):
        source = (my + groups - step) % groups
        rows = pl.ds(at * chunk, chunk)
        return pltpu.make_async_remote_copy(
            result.at[source, :, rows, :],
            out.at[:, rows, pl.ds(pl.multiple_of(source * LANES, LANES), LANES)],
            send_sem2.at[step, at],
            recv_sem2.at[step, at],
            (me, source),
            MESH,
        )

    for at in range(chunks):
        rows = slice(at * chunk, (at + 1) * chunk)
        terms = [
            lax.dot_general(
                across[m, rows, :], parts[m], (((1,), (1,)), ((), ())), preferred_element_type=jnp.float32
            )
            for m in range(4)
        ]
        even, odd = terms[0] + terms[2], terms[1] + terms[3]
        even_less, odd_less = terms[0] - terms[2], quarter_turn(terms[1] - terms[3])
        for g, value in enumerate([even + odd, even_less + odd_less, even - odd, even_less - odd_less]):
            for parity in range(2):
                result[g, parity, rows, :] = value[:, parity * LANES : (parity + 1) * LANES].astype(jnp.bfloat16)
        for step in (2, 1, 3):
            outgoing(step, at).start()
    mine = pltpu.make_async_copy(
        result.at[my], out.at[:, :, pl.ds(pl.multiple_of(my * LANES, LANES), LANES)], own_sem2
    )
    mine.start()

    def sent(step, carry):
        target = (me + step) % owners
        pltpu.make_async_remote_copy(
            blocks.at[target], place(me), send_sem.at[step], recv_sem.at[step], (target, my), MESH
        ).wait_send()
        return carry

    lax.fori_loop(1, owners, sent, 0)
    mine.wait()
    for at in range(chunks):
        for step in (1, 3, 2):
            incoming(step, at).wait_recv()
            outgoing(step, at).wait_send()


def finish(planes, rows, green, out):
    length = green.shape[1]
    totals = []
    for parity in range(2):
        plain = planes[parity]
        stacked = jnp.concatenate([plain, quarter_turn(plain.astype(jnp.float32)).astype(jnp.bfloat16)], 0)
        totals.append(jnp.dot(stacked, rows[parity], preferred_element_type=jnp.float32))
    count = planes.shape[1]
    for side, total in enumerate([totals[0] + totals[1], totals[0] - totals[1]]):
        columns = slice(side * length // 2, (side + 1) * length // 2)
        weights = green[:, columns].astype(jnp.float32)
        out[0, :, columns] = (weights * total[:count]).astype(jnp.bfloat16)
        out[1, :, columns] = (weights * total[count:]).astype(jnp.bfloat16)


def tables(owners, groups, edge, rows_brick, length):
    depth_cosine, depth_sine = wave(np.arange(owners), np.arange(BZ * edge), length, 1.0 / math.sqrt(BZ * edge))
    depth = np.concatenate([depth_cosine, -depth_sine], 0).reshape(2 * owners, BZ, edge).transpose(1, 0, 2)
    depth = np.concatenate([depth, depth], 2)
    i = np.arange(256)
    column, parity, x = i // 128, i // 64 % 2, i % 64
    weave = np.zeros((256, 256), np.float32)
    weave[i, parity * 128 + x % 4 * 32 + column * 16 + x // 4] = 1.0
    i = np.arange(512)
    gather = np.zeros((512, 512), np.float32)
    gather[i, i % 128 // 32 * 128 + i // 128 * 32 + i % 32] = 1.0
    across = []
    for m in range(4):
        cosine, sine = wave(np.arange(length // 4), 4 * np.arange(256) + m, length, 1.0 / math.sqrt(BX * edge))
        across.append(np.concatenate([cosine, sine], 1))
    brick_rows = owners * COL_DEV // BX
    rows = []
    for parity in range(2):
        g = np.arange(groups)[:, None, None]
        by = np.arange(brick_rows)[None, :, None]
        y = (by * edge + g * rows_brick + np.arange(rows_brick // 2)[None, None, :] * 2 + parity).reshape(groups, -1)
        pieces = []
        for group in range(groups):
            pieces += list(wave(y[group], np.arange(length // 2), length, 1.0 / math.sqrt(brick_rows * edge)))
        rows.append(np.concatenate(pieces, 0))
    return constant(depth), constant(weave), constant(gather), constant(np.stack(across)), constant(np.stack(rows))


def on_device(bricks, brick_coords, counts, green_kernel):
    _, kx_count, length = green_kernel.shape
    owners = lax.axis_size("wa")
    groups = lax.axis_size("gy")
    slots, edge, cells = bricks.shape
    rows_brick = cells // edge
    depth, weave, gather, across, rows = tables(owners, groups, edge, rows_brick, length)
    anywhere = pl.BlockSpec(memory_space=pl.ANY)
    scalars = pl.BlockSpec(memory_space=pltpu.SMEM)
    half = jnp.bfloat16
    planes = pl.pallas_call(
        exchange,
        out_shape=jax.ShapeDtypeStruct((2, kx_count, groups * LANES), half),
        in_specs=[scalars, scalars] + [anywhere] * 5,
        out_specs=pl.BlockSpec(memory_space=pltpu.VMEM),
        scratch_shapes=[
            pltpu.VMEM((slots * edge, cells), half),
            pltpu.VMEM(depth.shape, half),
            pltpu.VMEM(weave.shape, half),
            pltpu.VMEM(gather.shape, half),
            pltpu.VMEM(across.shape, half),
            pltpu.VMEM((2 * LANES, slots * edge), half),
            pltpu.VMEM((owners * 32, LANES), jnp.float32),
            pltpu.VMEM((owners, 2, 2, 8, LANES), half),
            pltpu.VMEM((2, 2, 64, BX * edge), half),
            pltpu.VMEM((4, 256, 512), half),
            pltpu.VMEM((groups, 2, length // 4, LANES), half),
            pltpu.SemaphoreType.DMA((5,)),
            pltpu.SemaphoreType.DMA((owners,)),
            pltpu.SemaphoreType.DMA((owners,)),
            pltpu.SemaphoreType.DMA(()),
            pltpu.SemaphoreType.DMA((groups, 4)),
            pltpu.SemaphoreType.DMA((groups, 4)),
            pltpu.SemaphoreType.DMA(()),
        ],
        compiler_params=pltpu.CompilerParams(
            collective_id=0, has_side_effects=True, vmem_limit_bytes=32 << 20
        ),
        name="exchange",
    )(brick_coords, counts, bricks.reshape(slots * edge, cells), depth, weave, gather, across)
    block = 128
    return pl.pallas_call(
        finish,
        out_shape=jax.ShapeDtypeStruct((2, kx_count, length), half),
        grid=(kx_count // block,),
        in_specs=[
            pl.BlockSpec((2, block, groups * LANES), lambda i: (0, i, 0)),
            pl.BlockSpec(rows.shape, lambda i: (0, 0, 0), pipeline_mode=pl.Buffered(1)),
            pl.BlockSpec((block, length), lambda i: (i, 0)),
        ],
        out_specs=pl.BlockSpec((2, block, length), lambda i: (0, i, 0)),
        compiler_params=pltpu.CompilerParams(vmem_limit_bytes=24 << 20),
        name="finish",
    )(planes, rows, green_kernel.reshape(kx_count, length))[None]


def solution(mesh):
    return jax.shard_map(
        on_device,
        mesh=mesh,
        in_specs=(P("wa", None, "gy"), P("wa", None), P("wa"), P("wa", "gy", None)),
        out_specs=P("wa", None, "gy", None),
        check_vma=False,
    )
```

time: 86.7 us -> 55.5 us (0.64)
  Pallas kernels: 0 us -> 47.7 us
  blocking collectives: 30.5 us -> 0 us
  matrix products: 20 us -> 0 us
  waiting for transfers between devices: 10.4 us -> 0 us
  local copies, waits for them, and re-layouts: 14.8 us -> 6.93 us
  other arithmetic: 5.76 us -> 0 us
  starting transfers between devices: 4.18 us -> 0 us
    pallas_call x0 -> x2, Pallas kernels: none -> 47.7 us  [the longest x1 43.2 us: on_device(): pl.pallas_call(exchange, out_shape=jax.ShapeDtypeStruct((2, kx_count, gro...]
    all_to_all x1 -> x0, blocking collectives: 30.5 us -> none  [on_device(): lax.all_to_all(spectra, 'wa', split_axis=0, concat_axis=0, tiled=True)]
    dot_general x3 -> x0, matrix products: 20 us -> none  [the longest x1 10.1 us: on_device(): jnp.einsum('pyx,opyr->oxr', regrouped, both, preferred_element_type=jnp.f...]
    all_to_all x1 -> x0, waiting for transfers between devices: 10.4 us -> none  [on_device(): lax.all_to_all(planes, 'gy', split_axis=2, concat_axis=1, tiled=True)]
    reshape x4 -> x0, local copies, waits for them, and re-layouts: 7.77 us -> none  [the longest x2 4.34 us: on_device(): sums.astype(jnp.bfloat16).reshape(COL_DEV, 2, depth_total, rows_brick, edge)]
    unnamed x2 -> x15, local copies, waits for them, and re-layouts: 0.01 us -> 6.93 us
    all_to_all x1 -> x0, starting transfers between devices: 4.18 us -> none  [on_device(): lax.all_to_all(planes, 'gy', split_axis=2, concat_axis=1, tiled=True)]
    mul x1 -> x0, other arithmetic: 4.06 us -> none  [on_device(): return (final * green_kernel.astype(jnp.float32)).astype(jnp.bfloat16)[None]]
  transfers between devices with their start and end apart: 1 -> 0, of which waited for: 1 -> 0; matrix products, arithmetic and copies ran while one was open for 5% -> 0% of each run, Pallas kernels for 0% -> 0%
where the time goes in v2:
time: 55.5 us; the launch traced here: 55.3 us
  Pallas kernels  47.7 us (86%)
  local copies, waits for them, and re-layouts  6.93 us (12%)
  between operations  0.68 us (1%)
    pallas_call x1, Pallas kernels, on_device(): pl.pallas_call(exchange, out_shape=jax.ShapeDtypeStruct((2, kx_count, gro...  43.2 us
    unnamed x15, local copies, waits for them, and re-layouts  6.93 us
    pallas_call x1, Pallas kernels, on_device(): pl.pallas_call(finish, out_shape=jax.ShapeDtypeStruct((2, kx_count, lengt...  4.49 us

profile of v2, /device:TPU:1, one launch (start us, length us, event | category | flops | bytes accessed | tf_op | source)
XLA Modules:
  0.0 55.3 jit_solution(12083436858721258563)
XLA Ops:
  0.7 0.8 %copy.10.coords = s32[16,2]{1,0:T(8,128)S(1)} copy(s32[16,2]{0,1:T(2,128)} %param.10) | data formatting | bytes 256 | tf_op args[1]
  1.4 0.0 copy-start
  1.4 1.6 %copy-done = bf16[16,64,1024]{2,1,0:T(8,128)(2,1)S(1)} copy-done((bf16[16,64,1024]{2,1,0:T(8,128)(2,1)S(1)}, bf16[16,64,1024]{2,1,0:T(8,128)(2,1)}, u32[]{:S(2)}) %copy-start) | copy-done | bytes 2097176
  3.0 0.0 copy-start.1
  3.0 1.6 %copy-done.1 = bf16[4,512,512]{2,1,0:T(8,128)(2,1)S(1)} copy-done((bf16[4,512,512]{2,1,0:T(8,128)(2,1)S(1)}, bf16[4,512,512]{2,1,0:T(8,128)(2,1)}, u32[]{:S(2)}) %copy-start.1) | copy-done | bytes 2097176
  4.6 0.0 copy-start.4
  4.6 1.0 %copy-done.4 = bf16[512,512]{1,0:T(8,128)(2,1)S(1)} copy-done((bf16[512,512]{1,0:T(8,128)(2,1)S(1)}, bf16[512,512]{1,0:T(8,128)(2,1)}, u32[]{:S(2)}) %copy-start.4) | copy-done | bytes 524312
  5.6 0.0 copy-start.5
  5.6 1.0 %copy-done.5 = bf16[16,128,128]{2,1,0:T(8,128)(2,1)S(1)} copy-done((bf16[16,128,128]{2,1,0:T(8,128)(2,1)S(1)}, bf16[16,128,128]{2,1,0:T(8,128)(2,1)}, u32[]{:S(2)}) %copy-start.5) | copy-done | bytes 524312
  6.7 0.0 copy-start.6
  6.7 0.9 %copy-done.6 = bf16[256,256]{1,0:T(8,128)(2,1)S(1)} copy-done((bf16[256,256]{1,0:T(8,128)(2,1)S(1)}, bf16[256,256]{1,0:T(8,128)(2,1)}, u32[]{:S(2)}) %copy-start.6) | copy-done | bytes 131096
  7.6 0.0 copy-start.2
  7.6 0.0 copy-start.3
  7.6 43.2 %exchange.1.planes = bf16[2,512,512]{2,1,0:T(8,128)(2,1)S(1)} custom-call(s32[16,2]{1,0:T(8,128)S(1)} %copy.10.coords, s32[1]{0:T(128)S(6)} %copy.11.counts, bf16[1024,1024]{1,0:T(8,128)(2,1)S(1)} %bitcast.3, bf16[16,128,128]{2,1,0:T(8,128)(2,1)S(1)} %copy-done.5, bf16[256,256]{1,0:T(8,128)(2,1)S(1)} %copy-done.6, bf16[512,512]{1,0:T(8,128)(2,1)S(1)} %copy-done.4, ...), custom_call_target="tpu_custom_call" | custom-call | tf_op jit(solution)/shard_map/exchange/pallas_call | solution.py:247
  50.8 0.0 copy-done.2
  50.8 0.0 copy-done.3
  50.8 4.5 %finish.1 = bf16[2,512,2048]{2,1,0:T(8,128)(2,1)} custom-call(bf16[2,512,512]{2,1,0:T(8,128)(2,1)S(1)} %exchange.1.planes, bf16[2,512,1024]{2,1,0:T(8,128)(2,1)S(1)} %copy-done.3, bf16[512,2048]{1,0:T(8,128)(2,1)S(1)} %bitcast.4), custom_call_target="tpu_custom_call" | custom-call | tf_op jit(solution)/shard_map/finish/pallas_call | solution.py:278
Async XLA Ops:
  1.4 1.6 %copy-start = (bf16[16,64,1024]{2,1,0:T(8,128)(2,1)S(1)}, bf16[16,64,1024]{2,1,0:T(8,128)(2,1)}, u32[]{:S(2)}) copy-start(bf16[16,64,1024]{2,1,0:T(8,128)(2,1)} %param.9) | copy-start | bytes 6291460
  3.0 1.6 %copy-start.1 = (bf16[4,512,512]{2,1,0:T(8,128)(2,1)S(1)}, bf16[4,512,512]{2,1,0:T(8,128)(2,1)}, u32[]{:S(2)}) copy-start(bf16[4,512,512]{2,1,0:T(8,128)(2,1)} %constant.13.clone.across_hbm) | copy-start | bytes 6291460
  4.6 1.0 %copy-start.4 = (bf16[512,512]{1,0:T(8,128)(2,1)S(1)}, bf16[512,512]{1,0:T(8,128)(2,1)}, u32[]{:S(2)}) copy-start(bf16[512,512]{1,0:T(8,128)(2,1)} %constant.12.clone.gather_hbm) | copy-start | bytes 1572868
  5.6 1.0 %copy-start.5 = (bf16[16,128,128]{2,1,0:T(8,128)(2,1)S(1)}, bf16[16,128,128]{2,1,0:T(8,128)(2,1)}, u32[]{:S(2)}) copy-start(bf16[16,128,128]{2,1,0:T(8,128)(2,1)} %constant.10.clone.depth_hbm) | copy-start | bytes 1572868
  6.7 0.9 %copy-start.6 = (bf16[256,256]{1,0:T(8,128)(2,1)S(1)}, bf16[256,256]{1,0:T(8,128)(2,1)}, u32[]{:S(2)}) copy-start(bf16[256,256]{1,0:T(8,128)(2,1)} %constant.11.clone.weave_hbm) | copy-start | bytes 393220
  7.6 43.2 %copy-start.2 = (bf16[1,512,2048]{2,1,0:T(8,128)(2,1)S(1)}, bf16[1,512,2048]{2,1,0:T(8,128)(2,1)}, u32[]{:S(2)}) copy-start(bf16[1,512,2048]{2,1,0:T(8,128)(2,1)} %param.12) | copy-start | bytes 6291460
  7.6 43.2 %copy-start.3 = (bf16[2,512,1024]{2,1,0:T(8,128)(2,1)S(1)}, bf16[2,512,1024]{2,1,0:T(8,128)(2,1)}, u32[]{:S(2)}) copy-start(bf16[2,512,1024]{2,1,0:T(8,128)(2,1)} %constant.14.clone.rows) | copy-start | bytes 6291460

commit v3 on v1

v3 whole, which is shorter than its diff:
```python
import math

import jax
import jax.numpy as jnp
import ml_dtypes
import numpy as np
from jax import lax
from jax.experimental import pallas as pl
from jax.experimental.pallas import tpu as pltpu
from jax.sharding import PartitionSpec as P

BX = 16
BZ = 16
COL_DEV = 2
MESH = pl.DeviceIdType.MESH
LANES = 128
PLANE = 8
GROUPS = 4


def wave(positions, frequency, length, factor):
    angles = (positions[:, None] * frequency[None, :] % length) * (2.0 * math.pi / length)
    return np.cos(angles) * factor, np.sin(angles) * factor


def constant(array):
    return jnp.asarray(array.astype(ml_dtypes.bfloat16))


def parity_half(group):
    return group % 2, group // 2


def unpack(planes):
    wide = planes.astype(jnp.float32)
    lane = lax.broadcasted_iota(jnp.int32, (1, LANES), 1)
    halves = [[], []]
    for at in range(0, wide.shape[1], 2 * LANES):
        left, right = wide[:, at : at + LANES], wide[:, at + LANES : at + 2 * LANES]
        halves[0].append(jnp.where(lane < 64, left, pltpu.roll(right, 64, 1)))
        halves[1].append(jnp.where(lane < 64, pltpu.roll(left, 64, 1), right))
    return [jnp.concatenate(pieces, 1).astype(jnp.bfloat16) for pieces in halves]


def exchange(
    coords, counts, bricks_hbm, depth_hbm, weave_hbm, gather_hbm, across_hbm, rows_hbm, last, even, odd,
    bricks, depth, weave, gather, across, rows, mixing, spread, blocks, relay, plane, parts, result, arrived,
    load_sem, send_a, recv_a, own_a, send_b, recv_b, own_b, send_c, recv_c, own_c,
):
    owners, groups = lax.axis_size("wa"), lax.axis_size("gy")
    levels = owners // PLANE
    me, my = lax.axis_index("wa"), lax.axis_index("gy")
    level, spot = me // PLANE, me % PLANE
    slots = coords.shape[1]
    half_cells = bricks.shape[2]

    def load(i):
        source, target = [
            (depth_hbm, depth),
            (bricks_hbm.at[:, pl.ds(0, half_cells)], bricks.at[0]),
            (bricks_hbm.at[:, pl.ds(half_cells, half_cells)], bricks.at[1]),
            (weave_hbm, weave),
            (gather_hbm, gather),
            (across_hbm, across),
            (rows_hbm, rows),
        ][i]
        return pltpu.make_async_copy(source, target, load_sem.at[i])

    for i in (0, 1, 3, 2):
        load(i).start()
    barrier = pltpu.get_barrier_semaphore()
    for step in range(1, PLANE):
        peer = level * PLANE + (spot + step) % PLANE
        pl.semaphore_signal(barrier, inc=1, device_id=(peer, my), device_id_type=MESH)
    for step in range(1, levels):
        peer = (level + step) % levels * PLANE + spot
        pl.semaphore_signal(barrier, inc=1, device_id=(peer, my), device_id_type=MESH)
    for step in range(1, groups):
        pl.semaphore_signal(barrier, inc=1, device_id=(me, (my + step) % groups), device_id_type=MESH)

    load(0).wait()
    lane = lax.broadcasted_iota(jnp.int32, (1, LANES), 1)
    for pair in range(slots // 2):
        first, second = 2 * pair, 2 * pair + 1
        picked = jnp.where(lane < 64, depth[coords[1, first]], depth[coords[1, second]])
        for column in range(COL_DEV):
            keep = [
                jnp.where(jnp.logical_and(coords[0, s] == column, s < counts[0]), 1.0, 0.0).astype(jnp.float32)
                for s in (first, second)
            ]
            mask = jnp.where(lane < 64, keep[0], keep[1]).astype(jnp.bfloat16)
            mixing[column * LANES : (column + 1) * LANES, pair * LANES : (pair + 1) * LANES] = picked * mask

    def own_copy_a(g):
        return pltpu.make_async_copy(
            blocks.at[g, :, spot], relay.at[g, :, :, pl.ds(pl.multiple_of(spot * LANES, LANES), LANES)], own_a.at[g]
        )

    def start_a(g):
        own_copy_a(g).start()
        for step in range(1, PLANE):
            target = (spot + step) % PLANE
            pltpu.make_async_remote_copy(
                blocks.at[g, :, target],
                relay.at[g, :, :, pl.ds(pl.multiple_of(spot * LANES, LANES), LANES)],
                send_a.at[g],
                recv_a.at[g],
                (level * PLANE + target, my),
                MESH,
            ).start()

    def own_copy_b(g):
        return pltpu.make_async_copy(relay.at[g, level], plane.at[g, level], own_b.at[g])

    def forward_b(g):
        own_copy_a(g).wait()
        seven = relay.at[g, pl.ds(0, PLANE - 1)]
        pltpu.make_async_copy(seven, seven, recv_a.at[g]).wait()
        for step in (4, 3, 5, 2, 6, 1, 7):
            target = (level + step) % levels
            pltpu.make_async_remote_copy(
                relay.at[g, target],
                plane.at[g, level],
                send_b.at[g],
                recv_b.at[g],
                (target * PLANE + spot, my),
                MESH,
            ).start()
        own_copy_b(g).start()

    for half in range(2):
        load(1 + half).wait()
        sums = jnp.dot(mixing[...], bricks[half], preferred_element_type=jnp.float32).astype(jnp.bfloat16)
        if half == 0:
            load(3).wait()
        lines = [
            jnp.concatenate([sums[:LANES, at : at + LANES], sums[LANES:, at : at + LANES]], 1)
            for at in range(0, half_cells, LANES)
        ]
        woven = jnp.dot(jnp.concatenate(lines, 0), weave[...], preferred_element_type=jnp.float32)
        for parity in range(2):
            g = half * 2 + parity
            for i in range(4):
                for part in range(2):
                    start = i * LANES + part * 64
                    spread[g, pl.ds(part * 4 + i, 64, stride=8), :] = woven[
                        start : start + 64, parity * LANES : (parity + 1) * LANES
                    ]
            blocks[g] = spread[g].astype(jnp.bfloat16).reshape(levels, PLANE, 8, LANES)
        if half == 0:
            pl.semaphore_wait(barrier, PLANE - 1 + levels - 1 + groups - 1)
        start_a(half * 2)
        start_a(half * 2 + 1)
    for i in (4, 5, 6):
        load(i).start()
    parts[...] = jnp.zeros_like(parts)
    for g in range(GROUPS):
        forward_b(g)

    def landing(g, source):
        columns = pl.ds(pl.multiple_of(source * LANES, LANES), LANES)
        return last.at[:, columns] if g == GROUPS - 1 else arrived.at[g, :, columns]

    def own_copy_c(g):
        return pltpu.make_async_copy(result.at[g, my], landing(g, my), own_c.at[g])

    def transform(g):
        own_copy_b(g).wait()
        seven = plane.at[g, pl.ds(0, levels - 1)]
        pltpu.make_async_copy(seven, seven, recv_b.at[g]).wait()
        if g == 0:
            load(4).wait()
        sign = jnp.where(lax.broadcasted_iota(jnp.int32, (8, 8, 512), 1) < 4, 1.0, -1.0)
        for half in range(2):
            piece = plane[g, :, :, half * 512 : (half + 1) * 512].reshape(64, 512)
            ordered = jnp.dot(piece, gather[...], preferred_element_type=jnp.float32)
            turned = (pltpu.roll(ordered.reshape(8, 8, 512), 4, 1) * sign).reshape(64, 512)
            at = half * LANES
            for m in range(4):
                columns = slice(m * LANES, (m + 1) * LANES)
                for high in range(2):
                    where = slice(high * 64, (high + 1) * 64)
                    parts[m, where, high * 512 + at : high * 512 + at + LANES] = ordered[:, columns].astype(jnp.bfloat16)
                    parts[m, where, high * 512 + 256 + at : high * 512 + 256 + at + LANES] = turned[:, columns].astype(
                        jnp.bfloat16
                    )
        if g == 0:
            load(5).wait()
        terms = [
            lax.dot_general(across[m], parts[m], (((1,), (1,)), ((), ())), preferred_element_type=jnp.float32)
            for m in range(4)
        ]
        both, less = terms[0] + terms[2], terms[0] - terms[2]
        odd_both, odd_less = terms[1] + terms[3], terms[1] - terms[3]
        turn = jnp.where(lane % 8 < 4, pltpu.roll(odd_less, LANES - 4, 1), -pltpu.roll(odd_less, 4, 1))
        for quarter, value in enumerate([both + odd_both, less + turn, both - odd_both, less - turn]):
            result[g, quarter] = value.astype(jnp.bfloat16)
        for step in (2, 1, 3):
            target = (my + step) % groups
            pltpu.make_async_remote_copy(
                result.at[g, target], landing(g, my), send_c.at[g], recv_c.at[g], (me, target), MESH
            ).start()
        own_copy_c(g).start()

    def landed(g):
        own_copy_c(g).wait()
        three = (last if g == GROUPS - 1 else arrived.at[g]).at[:, pl.ds(0, (groups - 1) * LANES)]
        pltpu.make_async_copy(three, three, recv_c.at[g]).wait()

    def gather_rows(g):
        landed(g)
        if g == 0:
            load(6).wait()
        parity, half = parity_half(g)
        total = odd if parity else even
        for high, value in enumerate(unpack(arrived[g])):
            where = slice(high * 256, (high + 1) * 256)
            for at in range(0, total.shape[1], 512):
                term = jnp.dot(value, rows[g, :, at : at + 512], preferred_element_type=jnp.float32)
                if half:
                    term = term + total[where, at : at + 512]
                total[where, at : at + 512] = term

    transform(0)
    transform(1)
    transform(2)
    gather_rows(0)
    transform(3)
    gather_rows(1)
    gather_rows(2)
    landed(3)
    for g in range(GROUPS):
        seven = blocks.at[g, pl.ds(0, PLANE - 1)]
        pltpu.make_async_copy(seven, seven, send_a.at[g]).wait()
        seven = relay.at[g, pl.ds(0, levels - 1)]
        pltpu.make_async_copy(seven, seven, send_b.at[g]).wait()
        three = result.at[g, pl.ds(0, groups - 1)]
        pltpu.make_async_copy(three, three, send_c.at[g]).wait()


def finish(last, even, odd, rows, green, out, block, sem):
    count, length = green.shape
    chunk = block.shape[2]
    wide = length // 4
    unpacked = unpack(last[...])
    copies = []
    for at in range(count // chunk):
        where = slice(at * chunk, (at + 1) * chunk)
        offset = at * chunk % 256
        value = unpacked[at * chunk // 256][offset : offset + chunk]
        for part in range(2):
            for piece in range(2):
                columns = slice(part * length // 2 + piece * wide, part * length // 2 + (piece + 1) * wide)
                term = jnp.dot(value, rows[:, columns], preferred_element_type=jnp.float32) + odd[where, columns]
                base = even[where, columns]
                for side, total in enumerate([base + term, base - term]):
                    start = side * length // 2 + piece * wide
                    weights = green[where, start : start + wide].astype(jnp.float32)
                    block[at, part, :, start : start + wide] = (weights * total).astype(jnp.bfloat16)
        copies.append(pltpu.make_async_copy(block.at[at], out.at[:, pl.ds(at * chunk, chunk), :], sem.at[at]))
        copies[-1].start()
    for copy in copies:
        copy.wait()


def tables(owners, groups, edge, rows_brick, length):
    depth_cosine, depth_sine = wave(np.arange(owners), np.arange(BZ * edge), length, 1.0 / math.sqrt(BZ * edge))
    depth = np.concatenate([depth_cosine, -depth_sine], 0).reshape(2 * owners, BZ, edge).transpose(1, 0, 2)
    depth = np.concatenate([depth, depth], 2)
    i = np.arange(256)
    column, parity, x = i // 128, i // 64 % 2, i % 64
    weave = np.zeros((256, 256), np.float32)
    weave[i, parity * 128 + x % 4 * 32 + column * 16 + x // 4] = 1.0
    i = np.arange(512)
    gather = np.zeros((512, 512), np.float32)
    gather[i, i % 128 // 32 * 128 + i // 128 * 32 + i % 32] = 1.0
    across = []
    for m in range(4):
        cosine, sine = wave(np.arange(length // 4), 4 * np.arange(256) + m, length, 1.0 / math.sqrt(BX * edge))
        both = np.concatenate([cosine, sine], 1)
        across.append(np.concatenate([both[:256], both[256:]], 1))
    brick_rows = owners * COL_DEV // BX
    rows = []
    for group in range(GROUPS):
        parity, half = parity_half(group)
        source = np.arange(groups)[:, None, None, None]
        by = np.arange(brick_rows)[None, :, None, None]
        part = np.arange(2)[None, None, :, None]
        line = np.arange(rows_brick // 4)[None, None, None, :]
        y = by * edge + source * rows_brick + (half * (rows_brick // 4) + line) * 2 + parity + 0 * part
        cosine, sine = wave(y.reshape(-1), np.arange(length // 2), length, 1.0 / math.sqrt(brick_rows * edge))
        imaginary = (part + 0 * y).reshape(-1)[:, None] == 1
        rows.append(np.concatenate([np.where(imaginary, sine, cosine), np.where(imaginary, cosine, -sine)], 1))
    return [constant(t) for t in (depth, weave, gather, np.stack(across), np.stack(rows[:-1]), rows[-1])]


def on_device(bricks, brick_coords, counts, green_kernel):
    _, kx_count, length = green_kernel.shape
    owners = lax.axis_size("wa")
    groups = lax.axis_size("gy")
    slots, edge, cells = bricks.shape
    rows_brick = cells // edge
    levels = owners // PLANE
    depth, weave, gather, across, rows, rows_last = tables(owners, groups, edge, rows_brick, length)
    in_place = pl.BlockSpec(memory_space=pltpu.HBM)
    scalars = pl.BlockSpec(memory_space=pltpu.SMEM)
    on_chip = pl.BlockSpec(memory_space=pltpu.VMEM)
    half = jnp.bfloat16
    copies = pltpu.SemaphoreType.DMA
    pinned = [
        pltpu.with_memory_space_constraint(v, pltpu.HBM)
        for v in (brick_coords.T, bricks.reshape(slots * edge, cells), depth, weave, gather, across, rows)
    ]
    last, even, odd = pl.pallas_call(
        exchange,
        out_shape=[
            jax.ShapeDtypeStruct((kx_count // 2, groups * LANES), half),
            jax.ShapeDtypeStruct((kx_count, length), jnp.float32),
            jax.ShapeDtypeStruct((kx_count, length), jnp.float32),
        ],
        in_specs=[scalars, scalars] + [in_place] * 6,
        out_specs=[on_chip] * 3,
        scratch_shapes=[
            pltpu.VMEM((2, slots * edge, cells // 2), half),
            pltpu.VMEM(depth.shape, half),
            pltpu.VMEM(weave.shape, half),
            pltpu.VMEM(gather.shape, half),
            pltpu.VMEM(across.shape, half),
            pltpu.VMEM(rows.shape, half),
            pltpu.VMEM((2 * LANES, slots * edge), half),
            pltpu.VMEM((GROUPS, owners * 8, LANES), jnp.float32),
            pltpu.VMEM((GROUPS, levels, PLANE, 8, LANES), half),
            pltpu.VMEM((GROUPS, levels, 8, BX * edge), half),
            pltpu.VMEM((GROUPS, levels, 8, BX * edge), half),
            pltpu.VMEM((4, LANES, 1024), half),
            pltpu.VMEM((GROUPS, groups, 256, LANES), half),
            pltpu.VMEM((GROUPS - 1, 256, groups * LANES), half),
            copies((7,)),
        ]
        + [copies((GROUPS,))] * 9,
        compiler_params=pltpu.CompilerParams(collective_id=0, has_side_effects=True, vmem_limit_bytes=36 << 20),
        name="exchange",
    )(pinned[0], counts, *pinned[1:])
    chunk = 128
    return pl.pallas_call(
        finish,
        out_shape=jax.ShapeDtypeStruct((2, kx_count, length), half),
        in_specs=[on_chip] * 5,
        out_specs=in_place,
        scratch_shapes=[pltpu.VMEM((kx_count // chunk, 2, chunk, length), half), copies((kx_count // chunk,))],
        compiler_params=pltpu.CompilerParams(vmem_limit_bytes=30 << 20),
        name="finish",
    )(last, even, odd, rows_last, green_kernel.reshape(kx_count, length))[None]


def solution(mesh):
    return jax.shard_map(
        on_device,
        mesh=mesh,
        in_specs=(P("wa", None, "gy"), P("wa", None), P("wa"), P("wa", "gy", None)),
        out_specs=P("wa", None, "gy", None),
        check_vma=False,
    )
```

time: 86.7 us -> 40 us (0.46)
  Pallas kernels: 0 us -> 39.2 us
  blocking collectives: 30.5 us -> 0 us
  matrix products: 20 us -> 0 us
  local copies, waits for them, and re-layouts: 14.8 us -> 0.01 us
  waiting for transfers between devices: 10.4 us -> 0 us
  other arithmetic: 5.76 us -> 0 us
  starting transfers between devices: 4.18 us -> 0 us
    pallas_call x0 -> x2, Pallas kernels: none -> 39.2 us  [the longest x1 36.5 us: on_device(): pl.pallas_call(exchange, out_shape=[jax.ShapeDtypeStruct((kx_count // 2,...]
    all_to_all x1 -> x0, blocking collectives: 30.5 us -> none  [on_device(): lax.all_to_all(spectra, 'wa', split_axis=0, concat_axis=0, tiled=True)]
    dot_general x3 -> x0, matrix products: 20 us -> none  [the longest x1 10.1 us: on_device(): jnp.einsum('pyx,opyr->oxr', regrouped, both, preferred_element_type=jnp.f...]
    all_to_all x1 -> x0, waiting for transfers between devices: 10.4 us -> none  [on_device(): lax.all_to_all(planes, 'gy', split_axis=2, concat_axis=1, tiled=True)]
    reshape x4 -> x0, local copies, waits for them, and re-layouts: 7.77 us -> none  [the longest x2 4.34 us: on_device(): sums.astype(jnp.bfloat16).reshape(COL_DEV, 2, depth_total, rows_brick, edge)]
    all_to_all x1 -> x0, starting transfers between devices: 4.18 us -> none  [on_device(): lax.all_to_all(planes, 'gy', split_axis=2, concat_axis=1, tiled=True)]
    mul x1 -> x0, other arithmetic: 4.06 us -> none  [on_device(): return (final * green_kernel.astype(jnp.float32)).astype(jnp.bfloat16)[None]]
    all_to_all x2 -> x0, local copies, waits for them, and re-layouts: 3.25 us -> none  [on_device(): lax.all_to_all(planes, 'gy', split_axis=2, concat_axis=1, tiled=True)]
  transfers between devices with their start and end apart: 1 -> 0, of which waited for: 1 -> 0; matrix products, arithmetic and copies ran while one was open for 5% -> 0% of each run, Pallas kernels for 0% -> 0%
where the time goes in v3:
time: 40 us; the launch traced here: 39.9 us
  Pallas kernels  39.2 us (98%)
  between operations  0.69 us (2%)
    pallas_call x1, Pallas kernels, on_device(): pl.pallas_call(exchange, out_shape=[jax.ShapeDtypeStruct((kx_count // 2,...  36.5 us
    pallas_call x1, Pallas kernels, on_device(): pl.pallas_call(finish, out_shape=jax.ShapeDtypeStruct((2, kx_count, lengt...  2.71 us

profile of v3, /device:TPU:1, one launch (start us, length us, event | category | flops | bytes accessed | tf_op | source)
XLA Modules:
  0.0 39.9 jit_solution(13972079810380089227)
XLA Ops:
  0.7 0.0 copy-start
  0.7 0.0 copy-start.1
  0.7 36.5 %exchange.1 = (bf16[256,512]{1,0:T(8,128)(2,1)S(1)}, f32[512,2048]{1,0:T(8,128)S(1)}, f32[512,2048]{1,0:T(8,128)S(1)}) custom-call(s32[2,16]{1,0:T(2,128)} %bitcast.6, s32[1]{0:T(128)S(6)} %copy.11.counts, bf16[1024,1024]{1,0:T(8,128)(2,1)} %bitcast.5, bf16[16,128,128]{2,1,0:T(8,128)(2,1)} %constant.12.clone.depth_hbm, ...), custom_call_target="tpu_custom_call" | custom-call | tf_op jit(solution)/shard_map/exchange/pallas_call | solution.py:314
  37.2 0.0 copy-done
  37.2 0.0 copy-done.1
  37.2 2.7 %finish.1 = bf16[2,512,2048]{2,1,0:T(8,128)(2,1)} custom-call(bf16[256,512]{1,0:T(8,128)(2,1)S(1)} %get-tuple-element.8.last, f32[512,2048]{1,0:T(8,128)S(1)} %get-tuple-element.9.even, f32[512,2048]{1,0:T(8,128)S(1)} %get-tuple-element.10.odd, bf16[256,2048]{1,0:T(8,128)(2,1)S(1)} %copy-done.1, bf16[512,2048]{1,0:T(8,128)(2,1)S(1)} %bitcast.4), custom_call_target="tpu_custom_call" | custom-call | tf_op jit(solution)/shard_map/finish/pallas_call | solution.py:345
Async XLA Ops:
  0.7 36.5 %copy-start = (bf16[1,512,2048]{2,1,0:T(8,128)(2,1)S(1)}, bf16[1,512,2048]{2,1,0:T(8,128)(2,1)}, u32[]{:S(2)}) copy-start(bf16[1,512,2048]{2,1,0:T(8,128)(2,1)} %param.13) | copy-start | bytes 6291460
  0.7 36.5 %copy-start.1 = (bf16[256,2048]{1,0:T(8,128)(2,1)S(1)}, bf16[256,2048]{1,0:T(8,128)(2,1)}, u32[]{:S(2)}) copy-start(bf16[256,2048]{1,0:T(8,128)(2,1)} %constant.17.clone.rows) | copy-start | bytes 3145732

commit v4 on v3

--- a/solution.py
+++ b/solution.py
@@ -15,6 +15,8 @@
 MESH = pl.DeviceIdType.MESH
 LANES = 128
 PLANE = 8
+SPLIT = 1
+LEVEL_FIRST = ()
 GROUPS = 4
 
 
@@ -43,9 +45,9 @@
 
 
 def exchange(
-    coords, counts, bricks_hbm, depth_hbm, weave_hbm, gather_hbm, across_hbm, rows_hbm, last, even, odd,
-    bricks, depth, weave, gather, across, rows, mixing, spread, blocks, relay, plane, parts, result, arrived,
-    load_sem, send_a, recv_a, own_a, send_b, recv_b, own_b, send_c, recv_c, own_c,
+    coords_hbm, counts, bricks_hbm, depth_hbm, weave_hbm, gather_hbm, across_hbm, rows_hbm, last, even, odd,
+    coords, bricks, depth, weave, gather, across, rows, mixing, spread, blocks, relay, middle, plane, parts, result, arrived,
+    load_sem, send_ab, recv_ab, send_c, recv_c,
 ):
     owners, groups = lax.axis_size("wa"), lax.axis_size("gy")
     levels = owners // PLANE
@@ -63,11 +65,24 @@
             (gather_hbm, gather),
             (across_hbm, across),
             (rows_hbm, rows),
+            (coords_hbm, coords),
         ][i]
         return pltpu.make_async_copy(source, target, load_sem.at[i])
 
-    for i in (0, 1, 3, 2):
+    def load_bricks(half):
+        step = bricks.shape[1] // 4
+        for at in range(0, bricks.shape[1], step):
+            pltpu.make_async_copy(
+                bricks_hbm.at[pl.ds(at, step), pl.ds(half * half_cells, half_cells)],
+                bricks.at[half, pl.ds(at, step)],
+                load_sem.at[1 + half],
+            ).start()
+
+    for i in (7, 0):
         load(i).start()
+    load_bricks(0)
+    load(3).start()
+    load_bricks(1)
     barrier = pltpu.get_barrier_semaphore()
     for step in range(1, PLANE):
         peer = level * PLANE + (spot + step) % PLANE
@@ -78,7 +93,8 @@
     for step in range(1, groups):
         pl.semaphore_signal(barrier, inc=1, device_id=(me, (my + step) % groups), device_id_type=MESH)
 
-    load(0).wait()
+    for i in (7, 0):
+        load(i).wait()
     lane = lax.broadcasted_iota(jnp.int32, (1, LANES), 1)
     for pair in range(slots // 2):
         first, second = 2 * pair, 2 * pair + 1
@@ -91,44 +107,40 @@
             mask = jnp.where(lane < 64, keep[0], keep[1]).astype(jnp.bfloat16)
             mixing[column * LANES : (column + 1) * LANES, pair * LANES : (pair + 1) * LANES] = picked * mask
 
-    def own_copy_a(g):
-        return pltpu.make_async_copy(
-            blocks.at[g, :, spot], relay.at[g, :, :, pl.ds(pl.multiple_of(spot * LANES, LANES), LANES)], own_a.at[g]
-        )
-
-    def start_a(g):
-        own_copy_a(g).start()
-        for step in range(1, PLANE):
-            target = (spot + step) % PLANE
+    def stripe(buffer, g):
+        return buffer.at[g, :, :, pl.ds(pl.multiple_of(spot * LANES, LANES), LANES)]
+
+    def pieces(g, second):
+        if (g in LEVEL_FIRST) == second:
+            source = (lambda target: middle.at[:, target]) if second else (lambda target: blocks.at[g, :, target])
+            return source, stripe(plane if second else relay, g), spot, PLANE, lambda t: level * PLANE + t
+        if second:
+            return lambda target: relay.at[g, target], plane.at[g, level], level, levels, lambda t: t * PLANE + spot
+        return lambda target: blocks.at[g, target], middle.at[level], level, levels, lambda t: t * PLANE + spot
+
+    def hop(g, second):
+        source, target, mine, count, device = pieces(g, second)
+        for step in (4, 3, 5, 2, 6, 1, 7):
+            peer = (mine + step) % count
             pltpu.make_async_remote_copy(
-                blocks.at[g, :, target],
-                relay.at[g, :, :, pl.ds(pl.multiple_of(spot * LANES, LANES), LANES)],
-                send_a.at[g],
-                recv_a.at[g],
-                (level * PLANE + target, my),
-                MESH,
+                source(peer), target, send_ab.at[int(second), g], recv_ab.at[int(second), g], (device(peer), my), MESH
             ).start()
-
-    def own_copy_b(g):
-        return pltpu.make_async_copy(relay.at[g, level], plane.at[g, level], own_b.at[g])
-
-    def forward_b(g):
-        own_copy_a(g).wait()
-        seven = relay.at[g, pl.ds(0, PLANE - 1)]
-        pltpu.make_async_copy(seven, seven, recv_a.at[g]).wait()
-        for step in (4, 3, 5, 2, 6, 1, 7):
-            target = (level + step) % levels
-            pltpu.make_async_remote_copy(
-                relay.at[g, target],
-                plane.at[g, level],
-                send_b.at[g],
-                recv_b.at[g],
-                (target * PLANE + spot, my),
-                MESH,
-            ).start()
-        own_copy_b(g).start()
-
-    for half in range(2):
+        target[...] = source(mine)[...]
+
+    def hop_landed(g, second):
+        buffer = plane.at[g] if second else middle if g in LEVEL_FIRST else relay.at[g]
+        seven = buffer.at[pl.ds(0, 7)]
+        pltpu.make_async_copy(seven, seven, recv_ab.at[int(second), g]).wait()
+
+    def hop_sent(g, second):
+        seven = plane.at[g, pl.ds(0, 7)]
+        pltpu.make_async_copy(seven, seven, send_ab.at[int(second), g]).wait()
+
+    def forward(g):
+        hop_landed(g, False)
+        hop(g, True)
+
+    def column_sums(half):
         load(1 + half).wait()
         sums = jnp.dot(mixing[...], bricks[half], preferred_element_type=jnp.float32).astype(jnp.bfloat16)
         if half == 0:
@@ -147,27 +159,13 @@
                         start : start + 64, parity * LANES : (parity + 1) * LANES
                     ]
             blocks[g] = spread[g].astype(jnp.bfloat16).reshape(levels, PLANE, 8, LANES)
-        if half == 0:
-            pl.semaphore_wait(barrier, PLANE - 1 + levels - 1 + groups - 1)
-        start_a(half * 2)
-        start_a(half * 2 + 1)
-    for i in (4, 5, 6):
-        load(i).start()
-    parts[...] = jnp.zeros_like(parts)
-    for g in range(GROUPS):
-        forward_b(g)
 
     def landing(g, source):
         columns = pl.ds(pl.multiple_of(source * LANES, LANES), LANES)
         return last.at[:, columns] if g == GROUPS - 1 else arrived.at[g, :, columns]
 
-    def own_copy_c(g):
-        return pltpu.make_async_copy(result.at[g, my], landing(g, my), own_c.at[g])
-
     def transform(g):
-        own_copy_b(g).wait()
-        seven = plane.at[g, pl.ds(0, levels - 1)]
-        pltpu.make_async_copy(seven, seven, recv_b.at[g]).wait()
+        hop_landed(g, True)
         if g == 0:
             load(4).wait()
         sign = jnp.where(lax.broadcasted_iota(jnp.int32, (8, 8, 512), 1) < 4, 1.0, -1.0)
@@ -200,10 +198,9 @@
             pltpu.make_async_remote_copy(
                 result.at[g, target], landing(g, my), send_c.at[g], recv_c.at[g], (me, target), MESH
             ).start()
-        own_copy_c(g).start()
+        landing(g, my)[...] = result[g, my]
 
     def landed(g):
-        own_copy_c(g).wait()
         three = (last if g == GROUPS - 1 else arrived.at[g]).at[:, pl.ds(0, (groups - 1) * LANES)]
         pltpu.make_async_copy(three, three, recv_c.at[g]).wait()
 
@@ -221,6 +218,20 @@
                     term = term + total[where, at : at + 512]
                 total[where, at : at + 512] = term
 
+    column_sums(0)
+    pl.semaphore_wait(barrier, PLANE - 1 + levels - 1 + groups - 1)
+    hop(0, False)
+    hop(1, False)
+    column_sums(1)
+    forward(0)
+    hop(2, False)
+    hop(3, False)
+    forward(1)
+    for i in (4, 5, 6):
+        load(i).start()
+    parts[...] = jnp.zeros_like(parts)
+    forward(2)
+    forward(3)
     transform(0)
     transform(1)
     transform(2)
@@ -230,10 +241,8 @@
     gather_rows(2)
     landed(3)
     for g in range(GROUPS):
-        seven = blocks.at[g, pl.ds(0, PLANE - 1)]
-        pltpu.make_async_copy(seven, seven, send_a.at[g]).wait()
-        seven = relay.at[g, pl.ds(0, levels - 1)]
-        pltpu.make_async_copy(seven, seven, send_b.at[g]).wait()
+        hop_sent(g, False)
+        hop_sent(g, True)
         three = result.at[g, pl.ds(0, groups - 1)]
         pltpu.make_async_copy(three, three, send_c.at[g]).wait()
 
@@ -257,8 +266,11 @@
                     start = side * length // 2 + piece * wide
                     weights = green[where, start : start + wide].astype(jnp.float32)
                     block[at, part, :, start : start + wide] = (weights * total).astype(jnp.bfloat16)
-        copies.append(pltpu.make_async_copy(block.at[at], out.at[:, pl.ds(at * chunk, chunk), :], sem.at[at]))
-        copies[-1].start()
+        for piece in range(SPLIT):
+            lines = pl.ds(piece * (chunk // SPLIT), chunk // SPLIT)
+            rows_out = pl.ds(at * chunk + piece * (chunk // SPLIT), chunk // SPLIT)
+            copies.append(pltpu.make_async_copy(block.at[at, :, lines], out.at[:, rows_out, :], sem.at[at, piece]))
+            copies[-1].start()
     for copy in copies:
         copy.wait()
 
@@ -318,9 +330,10 @@
             jax.ShapeDtypeStruct((kx_count, length), jnp.float32),
             jax.ShapeDtypeStruct((kx_count, length), jnp.float32),
         ],
-        in_specs=[scalars, scalars] + [in_place] * 6,
+        in_specs=[in_place, scalars] + [in_place] * 6,
         out_specs=[on_chip] * 3,
         scratch_shapes=[
+            pltpu.SMEM((COL_DEV, slots), jnp.int32),
             pltpu.VMEM((2, slots * edge, cells // 2), half),
             pltpu.VMEM(depth.shape, half),
             pltpu.VMEM(weave.shape, half),
@@ -331,13 +344,15 @@
             pltpu.VMEM((GROUPS, owners * 8, LANES), jnp.float32),
             pltpu.VMEM((GROUPS, levels, PLANE, 8, LANES), half),
             pltpu.VMEM((GROUPS, levels, 8, BX * edge), half),
+            pltpu.VMEM((levels, PLANE, 8, LANES), half),
             pltpu.VMEM((GROUPS, levels, 8, BX * edge), half),
             pltpu.VMEM((4, LANES, 1024), half),
             pltpu.VMEM((GROUPS, groups, 256, LANES), half),
             pltpu.VMEM((GROUPS - 1, 256, groups * LANES), half),
-            copies((7,)),
+            copies((8,)),
         ]
-        + [copies((GROUPS,))] * 9,
+        + [copies((2, GROUPS))] * 2
+        + [copies((GROUPS,))] * 2,
         compiler_params=pltpu.CompilerParams(collective_id=0, has_side_effects=True, vmem_limit_bytes=36 << 20),
         name="exchange",
     )(pinned[0], counts, *pinned[1:])
@@ -347,7 +362,7 @@
         out_shape=jax.ShapeDtypeStruct((2, kx_count, length), half),
         in_specs=[on_chip] * 5,
         out_specs=in_place,
-        scratch_shapes=[pltpu.VMEM((kx_count // chunk, 2, chunk, length), half), copies((kx_count // chunk,))],
+        scratch_shapes=[pltpu.VMEM((kx_count // chunk, 2, chunk, length), half), copies((kx_count // chunk, SPLIT))],
         compiler_params=pltpu.CompilerParams(vmem_limit_bytes=30 << 20),
         name="finish",
     )(last, even, odd, rows_last, green_kernel.reshape(kx_count, length))[None]

time: 40 us -> 37.5 us (0.938)
  Pallas kernels: 39.2 us -> 36.7 us
    pallas_call x1, Pallas kernels: 36.5 us -> 34 us  [on_device(): pl.pallas_call(exchange, out_shape=[jax.ShapeDtypeStruct((kx_count // 2,...]
where the time goes in v4:
time: 37.5 us; the launch traced here: 37.4 us
  Pallas kernels  36.7 us (98%)
  between operations  0.69 us (2%)
    pallas_call x1, Pallas kernels, on_device(): pl.pallas_call(exchange, out_shape=[jax.ShapeDtypeStruct((kx_count // 2,...  34 us
    pallas_call x1, Pallas kernels, on_device(): pl.pallas_call(finish, out_shape=jax.ShapeDtypeStruct((2, kx_count, lengt...  2.71 us

profile of v4, /device:TPU:1, one launch (start us, length us, event | category | flops | bytes accessed | tf_op | source)
XLA Modules:
  0.0 37.4 jit_solution(11448179659355536221)
XLA Ops:
  0.7 0.0 copy-start
  0.7 0.0 copy-start.1
  0.7 34.0 %exchange.1 = (bf16[256,512]{1,0:T(8,128)(2,1)S(1)}, f32[512,2048]{1,0:T(8,128)S(1)}, f32[512,2048]{1,0:T(8,128)S(1)}) custom-call(s32[2,16]{1,0:T(2,128)} %bitcast.6, s32[1]{0:T(128)S(6)} %copy.11.counts, bf16[1024,1024]{1,0:T(8,128)(2,1)} %bitcast.5, bf16[16,128,128]{2,1,0:T(8,128)(2,1)} %constant.12.clone.depth_hbm, ...), custom_call_target="tpu_custom_call" | custom-call | tf_op jit(solution)/shard_map/exchange/pallas_call | solution.py:326
  34.7 0.0 copy-done
  34.7 0.0 copy-done.1
  34.7 2.7 %finish.1 = bf16[2,512,2048]{2,1,0:T(8,128)(2,1)} custom-call(bf16[256,512]{1,0:T(8,128)(2,1)S(1)} %get-tuple-element.8.last, f32[512,2048]{1,0:T(8,128)S(1)} %get-tuple-element.9.even, f32[512,2048]{1,0:T(8,128)S(1)} %get-tuple-element.10.odd, bf16[256,2048]{1,0:T(8,128)(2,1)S(1)} %copy-done.1, bf16[512,2048]{1,0:T(8,128)(2,1)S(1)} %bitcast.4), custom_call_target="tpu_custom_call" | custom-call | tf_op jit(solution)/shard_map/finish/pallas_call | solution.py:360
Async XLA Ops:
  0.7 34.0 %copy-start = (bf16[1,512,2048]{2,1,0:T(8,128)(2,1)S(1)}, bf16[1,512,2048]{2,1,0:T(8,128)(2,1)}, u32[]{:S(2)}) copy-start(bf16[1,512,2048]{2,1,0:T(8,128)(2,1)} %param.13) | copy-start | bytes 6291460
  0.7 34.0 %copy-start.1 = (bf16[256,2048]{1,0:T(8,128)(2,1)S(1)}, bf16[256,2048]{1,0:T(8,128)(2,1)}, u32[]{:S(2)}) copy-start(bf16[256,2048]{1,0:T(8,128)(2,1)} %constant.17.clone.rows) | copy-start | bytes 3145732

commit v5 on v4

--- a/solution.py
+++ b/solution.py
@@ -16,7 +16,6 @@
 LANES = 128
 PLANE = 8
 SPLIT = 1
-LEVEL_FIRST = ()
 GROUPS = 4
 
 
@@ -46,13 +45,14 @@
 
 def exchange(
     coords_hbm, counts, bricks_hbm, depth_hbm, weave_hbm, gather_hbm, across_hbm, rows_hbm, last, even, odd,
-    coords, bricks, depth, weave, gather, across, rows, mixing, spread, blocks, relay, middle, plane, parts, result, arrived,
-    load_sem, send_ab, recv_ab, send_c, recv_c,
+    coords, bricks, depth, weave, gather, across, rows, mixing, spread, blocks, paired, plane, parts, result, arrived,
+    load_sem, send_p, recv_p, send_c, recv_c,
 ):
     owners, groups = lax.axis_size("wa"), lax.axis_size("gy")
     levels = owners // PLANE
     me, my = lax.axis_index("wa"), lax.axis_index("gy")
     level, spot = me // PLANE, me % PLANE
+    across_x, core = spot // 2, spot % 2
     slots = coords.shape[1]
     half_cells = bricks.shape[2]
 
@@ -84,15 +84,17 @@
     load(3).start()
     load_bricks(1)
     barrier = pltpu.get_barrier_semaphore()
-    for step in range(1, PLANE):
-        peer = level * PLANE + (spot + step) % PLANE
-        pl.semaphore_signal(barrier, inc=1, device_id=(peer, my), device_id_type=MESH)
-    for step in range(1, levels):
-        peer = (level + step) % levels * PLANE + spot
-        pl.semaphore_signal(barrier, inc=1, device_id=(peer, my), device_id_type=MESH)
+    peer = level * PLANE + across_x * 2 + 1 - core
+    pl.semaphore_signal(barrier, inc=1, device_id=(peer, my), device_id_type=MESH)
+    for step in range(levels):
+        for step_x in range(PLANE // 2):
+            if step + step_x > 0:
+                peer = (level + step) % levels * PLANE + (across_x + step_x) % (PLANE // 2) * 2 + core
+                pl.semaphore_signal(barrier, inc=1, device_id=(peer, my), device_id_type=MESH)
     for step in range(1, groups):
         pl.semaphore_signal(barrier, inc=1, device_id=(me, (my + step) % groups), device_id_type=MESH)
 
+    parts[...] = jnp.zeros_like(parts)
     for i in (7, 0):
         load(i).wait()
     lane = lax.broadcasted_iota(jnp.int32, (1, LANES), 1)
@@ -107,38 +109,35 @@
             mask = jnp.where(lane < 64, keep[0], keep[1]).astype(jnp.bfloat16)
             mixing[column * LANES : (column + 1) * LANES, pair * LANES : (pair + 1) * LANES] = picked * mask
 
-    def stripe(buffer, g):
-        return buffer.at[g, :, :, pl.ds(pl.multiple_of(spot * LANES, LANES), LANES)]
-
-    def pieces(g, second):
-        if (g in LEVEL_FIRST) == second:
-            source = (lambda target: middle.at[:, target]) if second else (lambda target: blocks.at[g, :, target])
-            return source, stripe(plane if second else relay, g), spot, PLANE, lambda t: level * PLANE + t
-        if second:
-            return lambda target: relay.at[g, target], plane.at[g, level], level, levels, lambda t: t * PLANE + spot
-        return lambda target: blocks.at[g, target], middle.at[level], level, levels, lambda t: t * PLANE + spot
-
-    def hop(g, second):
-        source, target, mine, count, device = pieces(g, second)
-        for step in (4, 3, 5, 2, 6, 1, 7):
-            peer = (mine + step) % count
-            pltpu.make_async_remote_copy(
-                source(peer), target, send_ab.at[int(second), g], recv_ab.at[int(second), g], (device(peer), my), MESH
-            ).start()
-        target[...] = source(mine)[...]
-
-    def hop_landed(g, second):
-        buffer = plane.at[g] if second else middle if g in LEVEL_FIRST else relay.at[g]
-        seven = buffer.at[pl.ds(0, 7)]
-        pltpu.make_async_copy(seven, seven, recv_ab.at[int(second), g]).wait()
-
-    def hop_sent(g, second):
-        seven = plane.at[g, pl.ds(0, 7)]
-        pltpu.make_async_copy(seven, seven, send_ab.at[int(second), g]).wait()
-
-    def forward(g):
-        hop_landed(g, False)
-        hop(g, True)
+    def half_lines(g):
+        return paired.at[g, :, :, :, pl.ds(pl.multiple_of(core * LANES, LANES), LANES)]
+
+    def core_hop(g):
+        pltpu.make_async_remote_copy(
+            blocks.at[g, :, :, 1 - core],
+            half_lines(g),
+            send_p.at[0, g],
+            recv_p.at[0, g],
+            (level * PLANE + across_x * 2 + 1 - core, my),
+            MESH,
+        ).start()
+        half_lines(g)[...] = blocks[g, :, :, core]
+
+    def core_forward(g):
+        lines = paired.at[g, :, :, :, pl.ds(0, LANES)]
+        pltpu.make_async_copy(lines, lines, recv_p.at[0, g]).wait()
+        target = plane.at[g, level, :, pl.ds(pl.multiple_of(across_x * 2 * LANES, 2 * LANES), 2 * LANES)]
+        for step_x in (2, 1, 3, 0):
+            for step_z in (4, 3, 5, 2, 6, 1, 7, 0):
+                if step_z + step_x > 0:
+                    z, x = (level + step_z) % levels, (across_x + step_x) % (PLANE // 2)
+                    pltpu.make_async_remote_copy(
+                        paired.at[g, z, x], target, send_p.at[1, g], recv_p.at[1, g], (z * PLANE + x * 2 + core, my), MESH
+                    ).start()
+        target[...] = paired[g, level, across_x]
+
+    def core_bytes(g):
+        return spread.at[g, pl.ds(0, (owners // 2 - 1) * 8)]
 
     def column_sums(half):
         load(1 + half).wait()
@@ -158,14 +157,14 @@
                     spread[g, pl.ds(part * 4 + i, 64, stride=8), :] = woven[
                         start : start + 64, parity * LANES : (parity + 1) * LANES
                     ]
-            blocks[g] = spread[g].astype(jnp.bfloat16).reshape(levels, PLANE, 8, LANES)
+            blocks[g] = spread[g].astype(jnp.bfloat16).reshape(levels, PLANE // 2, 2, 8, LANES)
 
     def landing(g, source):
         columns = pl.ds(pl.multiple_of(source * LANES, LANES), LANES)
         return last.at[:, columns] if g == GROUPS - 1 else arrived.at[g, :, columns]
 
     def transform(g):
-        hop_landed(g, True)
+        pltpu.make_async_copy(core_bytes(g), core_bytes(g), recv_p.at[1, g]).wait()
         if g == 0:
             load(4).wait()
         sign = jnp.where(lax.broadcasted_iota(jnp.int32, (8, 8, 512), 1) < 4, 1.0, -1.0)
@@ -219,20 +218,19 @@
                 total[where, at : at + 512] = term
 
     column_sums(0)
-    pl.semaphore_wait(barrier, PLANE - 1 + levels - 1 + groups - 1)
-    hop(0, False)
-    hop(1, False)
+    pl.semaphore_wait(barrier, 1 + owners // 2 - 1 + groups - 1)
+    core_hop(0)
+    core_hop(1)
     column_sums(1)
-    forward(0)
-    hop(2, False)
-    hop(3, False)
-    forward(1)
+    core_hop(2)
+    core_hop(3)
     for i in (4, 5, 6):
         load(i).start()
-    parts[...] = jnp.zeros_like(parts)
-    forward(2)
-    forward(3)
+    core_forward(0)
+    core_forward(1)
+    core_forward(2)
     transform(0)
+    core_forward(3)
     transform(1)
     transform(2)
     gather_rows(0)
@@ -241,8 +239,9 @@
     gather_rows(2)
     landed(3)
     for g in range(GROUPS):
-        hop_sent(g, False)
-        hop_sent(g, True)
+        lines = paired.at[g, :, :, :, pl.ds(0, LANES)]
+        pltpu.make_async_copy(lines, lines, send_p.at[0, g]).wait()
+        pltpu.make_async_copy(core_bytes(g), core_bytes(g), send_p.at[1, g]).wait()
         three = result.at[g, pl.ds(0, groups - 1)]
         pltpu.make_async_copy(three, three, send_c.at[g]).wait()
 
@@ -342,9 +341,8 @@
             pltpu.VMEM(rows.shape, half),
             pltpu.VMEM((2 * LANES, slots * edge), half),
             pltpu.VMEM((GROUPS, owners * 8, LANES), jnp.float32),
-            pltpu.VMEM((GROUPS, levels, PLANE, 8, LANES), half),
-            pltpu.VMEM((GROUPS, levels, 8, BX * edge), half),
-            pltpu.VMEM((levels, PLANE, 8, LANES), half),
+            pltpu.VMEM((GROUPS, levels, PLANE // 2, 2, 8, LANES), half),
+            pltpu.VMEM((GROUPS, levels, PLANE // 2, 8, 2 * LANES), half),
             pltpu.VMEM((GROUPS, levels, 8, BX * edge), half),
             pltpu.VMEM((4, LANES, 1024), half),
             pltpu.VMEM((GROUPS, groups, 256, LANES), half),

time: 37.5 us -> 36.4 us (0.971)
  Pallas kernels: 36.7 us -> 35.6 us
    pallas_call x1, Pallas kernels: 34 us -> 32.9 us  [on_device(): pl.pallas_call(exchange, out_shape=[jax.ShapeDtypeStruct((kx_count // 2,...]
where the time goes in v5:
time: 36.4 us; the launch traced here: 36.3 us
  Pallas kernels  35.6 us (98%)
  between operations  0.69 us (2%)
    pallas_call x1, Pallas kernels, on_device(): pl.pallas_call(exchange, out_shape=[jax.ShapeDtypeStruct((kx_count // 2,...  32.9 us
    pallas_call x1, Pallas kernels, on_device(): pl.pallas_call(finish, out_shape=jax.ShapeDtypeStruct((2, kx_count, lengt...  2.71 us

profile of v5, /device:TPU:1, one launch (start us, length us, event | category | flops | bytes accessed | tf_op | source)
XLA Modules:
  0.0 36.3 jit_solution(11816770505804606553)
XLA Ops:
  0.7 0.0 copy-start
  0.7 0.0 copy-start.1
  0.7 32.9 %exchange.1 = (bf16[256,512]{1,0:T(8,128)(2,1)S(1)}, f32[512,2048]{1,0:T(8,128)S(1)}, f32[512,2048]{1,0:T(8,128)S(1)}) custom-call(s32[2,16]{1,0:T(2,128)} %bitcast.6, s32[1]{0:T(128)S(6)} %copy.11.counts, bf16[1024,1024]{1,0:T(8,128)(2,1)} %bitcast.5, bf16[16,128,128]{2,1,0:T(8,128)(2,1)} %constant.12.clone.depth_hbm, ...), custom_call_target="tpu_custom_call" | custom-call | tf_op jit(solution)/shard_map/exchange/pallas_call | solution.py:325
  33.6 0.0 copy-done
  33.6 0.0 copy-done.1
  33.6 2.7 %finish.1 = bf16[2,512,2048]{2,1,0:T(8,128)(2,1)} custom-call(bf16[256,512]{1,0:T(8,128)(2,1)S(1)} %get-tuple-element.8.last, f32[512,2048]{1,0:T(8,128)S(1)} %get-tuple-element.9.even, f32[512,2048]{1,0:T(8,128)S(1)} %get-tuple-element.10.odd, bf16[256,2048]{1,0:T(8,128)(2,1)S(1)} %copy-done.1, bf16[512,2048]{1,0:T(8,128)(2,1)S(1)} %bitcast.4), custom_call_target="tpu_custom_call" | custom-call | tf_op jit(solution)/shard_map/finish/pallas_call | solution.py:358
Async XLA Ops:
  0.7 33.0 %copy-start = (bf16[1,512,2048]{2,1,0:T(8,128)(2,1)S(1)}, bf16[1,512,2048]{2,1,0:T(8,128)(2,1)}, u32[]{:S(2)}) copy-start(bf16[1,512,2048]{2,1,0:T(8,128)(2,1)} %param.13) | copy-start | bytes 6291460
  0.7 33.0 %copy-start.1 = (bf16[256,2048]{1,0:T(8,128)(2,1)S(1)}, bf16[256,2048]{1,0:T(8,128)(2,1)}, u32[]{:S(2)}) copy-start(bf16[256,2048]{1,0:T(8,128)(2,1)} %constant.17.clone.rows) | copy-start | bytes 3145732

commit v6 on v5

--- a/solution.py
+++ b/solution.py
@@ -192,7 +192,7 @@
         turn = jnp.where(lane % 8 < 4, pltpu.roll(odd_less, LANES - 4, 1), -pltpu.roll(odd_less, 4, 1))
         for quarter, value in enumerate([both + odd_both, less + turn, both - odd_both, less - turn]):
             result[g, quarter] = value.astype(jnp.bfloat16)
-        for step in (2, 1, 3):
+        for step in (1, 3, 2):
             target = (my + step) % groups
             pltpu.make_async_remote_copy(
                 result.at[g, target], landing(g, my), send_c.at[g], recv_c.at[g], (me, target), MESH

time: 36.4 us -> 36.1 us (level)
  no operation moved by 1% of the time
where the time goes in v6:
time: 36.1 us
  Pallas kernels  35.4 us (98%)
  between operations  0.69 us (2%)
    pallas_call x1, Pallas kernels, on_device(): pl.pallas_call(exchange, out_shape=[jax.ShapeDtypeStruct((kx_count // 2,...  32.6 us
    pallas_call x1, Pallas kernels, on_device(): pl.pallas_call(finish, out_shape=jax.ShapeDtypeStruct((2, kx_count, lengt...  2.71 us

profile of v6, /device:TPU:1, one launch (start us, length us, event | category | flops | bytes accessed | tf_op | source)
XLA Modules:
  0.0 36.1 jit_solution(1920259333269036047)
XLA Ops:
  0.7 0.0 copy-start
  0.7 0.0 copy-start.1
  0.7 32.6 %exchange.1 = (bf16[256,512]{1,0:T(8,128)(2,1)S(1)}, f32[512,2048]{1,0:T(8,128)S(1)}, f32[512,2048]{1,0:T(8,128)S(1)}) custom-call(s32[2,16]{1,0:T(2,128)} %bitcast.6, s32[1]{0:T(128)S(6)} %copy.11.counts, bf16[1024,1024]{1,0:T(8,128)(2,1)} %bitcast.5, bf16[16,128,128]{2,1,0:T(8,128)(2,1)} %constant.12.clone.depth_hbm, ...), custom_call_target="tpu_custom_call" | custom-call | tf_op jit(solution)/shard_map/exchange/pallas_call | solution.py:325
  33.3 0.0 copy-done
  33.3 0.0 copy-done.1
  33.4 2.7 %finish.1 = bf16[2,512,2048]{2,1,0:T(8,128)(2,1)} custom-call(bf16[256,512]{1,0:T(8,128)(2,1)S(1)} %get-tuple-element.8.last, f32[512,2048]{1,0:T(8,128)S(1)} %get-tuple-element.9.even, f32[512,2048]{1,0:T(8,128)S(1)} %get-tuple-element.10.odd, bf16[256,2048]{1,0:T(8,128)(2,1)S(1)} %copy-done.1, bf16[512,2048]{1,0:T(8,128)(2,1)S(1)} %bitcast.4), custom_call_target="tpu_custom_call" | custom-call | tf_op jit(solution)/shard_map/finish/pallas_call | solution.py:358
Async XLA Ops:
  0.7 32.7 %copy-start = (bf16[1,512,2048]{2,1,0:T(8,128)(2,1)S(1)}, bf16[1,512,2048]{2,1,0:T(8,128)(2,1)}, u32[]{:S(2)}) copy-start(bf16[1,512,2048]{2,1,0:T(8,128)(2,1)} %param.13) | copy-start | bytes 6291460
  0.7 32.7 %copy-start.1 = (bf16[256,2048]{1,0:T(8,128)(2,1)S(1)}, bf16[256,2048]{1,0:T(8,128)(2,1)}, u32[]{:S(2)}) copy-start(bf16[256,2048]{1,0:T(8,128)(2,1)} %constant.17.clone.rows) | copy-start | bytes 3145732
